TPU v7x, 32 devices: a whole 2x2x4 slice. The times are simulated.
32 devices in a mesh: fsdp: 8 (over z, x), seq: 4 (over y, core).
Axes of the slice: x: 2, y: 2, z: 4, core: 2. Of those that a mesh axis runs over, the one named last changes fastest.
Arguments:
- tokens: bfloat16 [8, 1536, 1024], P('fsdp', 'seq'), may hold values from -6 to 6
- doc_starts: int32 [8, 1536], P('fsdp', 'seq'), may hold values from 0 to 1, as said below
- qkv_weight: bfloat16 [1024, 3072], P('fsdp'), may hold values from -0.1875 to 0.1875
- query_bias: bfloat16 [1024], P('fsdp'), may hold values from -1.5 to 1.5
- value_bias: bfloat16 [1024], P('fsdp'), may hold values from -0.5 to 0.5
- out_weight: bfloat16 [1024, 1024], P('fsdp'), may hold values from -1.5 to 1.5
- out_bias: bfloat16 [1024], P('fsdp'), may hold values from -1.5 to 1.5
- norm1_gain: bfloat16 [1024], P('fsdp'), may hold values from 0.5 to 1.5
- norm1_shift: bfloat16 [1024], P('fsdp'), may hold values from -1.5 to 1.5
- up_weight: bfloat16 [1024, 4096], P('fsdp'), may hold values from -0.1875 to 0.1875
- up_bias: bfloat16 [4096], P('fsdp'), may hold values from -1.5 to 1.5
- down_weight: bfloat16 [4096, 1024], P('fsdp'), may hold values from -0.09375 to 0.09375
- down_bias: bfloat16 [1024], P('fsdp'), may hold values from -1.5 to 1.5
- norm2_gain: bfloat16 [1024], P('fsdp'), may hold values from 0.5 to 1.5
- norm2_shift: bfloat16 [1024], P('fsdp'), may hold values from -1.5 to 1.5
- cotangent: bfloat16 [8, 1536, 1024], P('fsdp', 'seq'), may hold values from -6 to 6
Outputs:
- layer_out: bfloat16 [8, 1536, 1024], P('fsdp', 'seq')
- input_grad: float32 [8, 1536, 1024], P('fsdp', 'seq')
- qkv_weight_grad: float32 [1024, 3072], P('fsdp')
- query_bias_grad: float32 [1024], P('fsdp')
- value_bias_grad: float32 [1024], P('fsdp')
- out_weight_grad: float32 [1024, 1024], P('fsdp')
- out_bias_grad: float32 [1024], P('fsdp')
- norm1_gain_grad: float32 [1024], P('fsdp')
- norm1_shift_grad: float32 [1024], P('fsdp')
- up_weight_grad: float32 [1024, 4096], P('fsdp')
- up_bias_grad: float32 [4096], P('fsdp')
- down_weight_grad: float32 [4096, 1024], P('fsdp')
- down_bias_grad: float32 [1024], P('fsdp')
- norm2_gain_grad: float32 [1024], P('fsdp')
- norm2_shift_grad: float32 [1024], P('fsdp')
Inputs may be any that keep to these rules, and one draw needn't show every extreme that they name: `doc_starts`: each row's first token starts a document; every document has at most 512 tokens, and each row holds at least one document of exactly 512 tokens.
All inputs are finite; a program needn't handle non-finite values.
Results may differ from a plain program's by a relative error of at most 0.014.
The roundings to bfloat16 on the way count: a program that leaves them out, or rounds other values in their place, can miss the bound.
Values may be sent and summed in bfloat16 or wider, within the bound.
No kernel may reach another device: no remote copies, remote signals or barrier semaphores. Data moves between devices by JAX's collectives and lax.ppermute only.
A program may use at most 192 MiB of HBM per device.

v0:
```python
import jax
import jax.numpy as jnp
from jax import lax
from jax.sharding import PartitionSpec as P

D = 1024
HD = 64
QBLOCK = 512


EPSILON = 1e-05


def carried_in(value, axis, join, neutral):
    count, mine = (lax.axis_size(axis), lax.axis_index(axis))
    pieces = lax.all_gather(value, axis)
    total = jnp.full_like(value, 0) + jnp.asarray(neutral, value.dtype)

    def turn(position, total):
        longer = join(total, pieces[position])
        return jnp.where(position < mine, longer, total)

    return lax.fori_loop(0, count - 1, turn, total)


def contract_rows(left, right):
    return lax.dot_general(
        left, right, (((0,), (0,)), ((), ())), preferred_element_type=jnp.float32
    )


def contract_cols(left, right):
    return lax.dot_general(
        left, right, (((1,), (1,)), ((), ())), preferred_element_type=jnp.float32
    )


def exact_gelu(values):
    return jax.nn.gelu(values, approximate=False)


def normalize(hidden, gain, shift):
    center = hidden - jnp.mean(hidden, axis=-1, keepdims=True)
    inverse = lax.rsqrt(jnp.mean(center * center, axis=-1, keepdims=True) + EPSILON)
    normed = center * inverse
    return (normed * gain + shift, normed, inverse)


def norm_back(incoming, normed, inverse, gain):
    scaled = incoming * gain
    d_hidden = inverse * (
        scaled
        - jnp.mean(scaled, axis=-1, keepdims=True)
        - normed * jnp.mean(scaled * normed, axis=-1, keepdims=True)
    )
    return (d_hidden, jnp.sum(incoming * normed, axis=0), jnp.sum(incoming, axis=0))


def masked_scores(query_block, segment_block, key_rows, segment, scale):
    scores = (
        jnp.einsum("qhd,khd->hqk", query_block, key_rows, preferred_element_type=jnp.float32)
        * scale
    )
    allowed = (segment_block[:, None] == segment[None, :])[None]
    return jnp.where(allowed, scores, -jnp.inf)


def attend(head_query, head_key, head_value, segment):
    length = head_query.shape[0]
    heads = head_query.shape[1] // HD
    blocks = length // QBLOCK
    scale = HD ** (-0.5)
    key_rows = head_key.reshape(length, heads, HD)
    value_rows = head_value.reshape(length, heads, HD)
    query_blocks = head_query.reshape(blocks, QBLOCK, heads, HD)
    segment_blocks = segment.reshape(blocks, QBLOCK)

    def one_block(carry, pair):
        query_block, segment_block = pair
        scores = masked_scores(query_block, segment_block, key_rows, segment, scale)
        highest = jnp.max(scores, axis=-1, keepdims=True)
        exponent = jnp.exp(scores - highest)
        total = jnp.sum(exponent, axis=-1, keepdims=True)
        weights = (exponent / total).astype(jnp.bfloat16)
        context = jnp.einsum(
            "hqk,khd->qhd", weights, value_rows, preferred_element_type=jnp.float32
        )
        context = context.astype(jnp.bfloat16).reshape(QBLOCK, heads * HD)
        return (carry, (context, (highest + jnp.log(total))[..., 0]))

    unused, (context, log_total) = lax.scan(one_block, 0, (query_blocks, segment_blocks))
    return (context.reshape(length, heads * HD), log_total)


def attend_back(head_query, head_key, head_value, segment, log_total, head_grad):
    length = head_query.shape[0]
    heads = head_query.shape[1] // HD
    blocks = length // QBLOCK
    scale = HD ** (-0.5)
    key_rows = head_key.reshape(length, heads, HD)
    value_rows = head_value.reshape(length, heads, HD)
    query_blocks = head_query.reshape(blocks, QBLOCK, heads, HD)
    grad_blocks = head_grad.reshape(blocks, QBLOCK, heads, HD)
    segment_blocks = segment.reshape(blocks, QBLOCK)

    def one_block(carry, group):
        sum_key, sum_value = carry
        query_block, segment_block, total_block, grad_block = group
        scores = masked_scores(query_block, segment_block, key_rows, segment, scale)
        probs = jnp.exp(scores - total_block[..., None])
        d_probs = jnp.einsum(
            "qhd,khd->hqk", grad_block, value_rows, preferred_element_type=jnp.float32
        )
        centre = jnp.sum(probs * d_probs, axis=-1, keepdims=True)
        d_scores = (probs * (d_probs - centre)).astype(jnp.bfloat16)
        d_query = (
            jnp.einsum("hqk,khd->qhd", d_scores, key_rows, preferred_element_type=jnp.float32)
            * scale
        )
        sum_key = (
            sum_key
            + jnp.einsum("hqk,qhd->khd", d_scores, query_block, preferred_element_type=jnp.float32)
            * scale
        )
        sum_value = sum_value + jnp.einsum(
            "hqk,qhd->khd",
            probs.astype(jnp.bfloat16),
            grad_block,
            preferred_element_type=jnp.float32,
        )
        return ((sum_key, sum_value), d_query.astype(jnp.bfloat16).reshape(QBLOCK, heads * HD))

    zeros = jnp.zeros((length, heads, HD), jnp.float32)
    (sum_key, sum_value), d_query = lax.scan(
        one_block, (zeros, zeros), (query_blocks, segment_blocks, log_total, grad_blocks)
    )
    return (
        d_query.reshape(length, heads * HD),
        sum_key.reshape(length, heads * HD).astype(jnp.bfloat16),
        sum_value.reshape(length, heads * HD).astype(jnp.bfloat16),
    )


def body(
    tokens,
    doc_starts,
    qkv_weight,
    query_bias,
    value_bias,
    out_weight,
    out_bias,
    norm1_gain,
    norm1_shift,
    up_weight,
    up_bias,
    down_weight,
    down_bias,
    norm2_gain,
    norm2_shift,
    cotangent,
):
    shards = (
        qkv_weight,
        query_bias,
        value_bias,
        out_weight,
        out_bias,
        norm1_gain,
        norm1_shift,
        up_weight,
        up_bias,
        down_weight,
        down_bias,
        norm2_gain,
        norm2_shift,
    )
    gathered = (
        lax.all_gather(shards[0], "fsdp", axis=0, tiled=True),
        lax.all_gather(shards[1], "fsdp", axis=0, tiled=True),
        lax.all_gather(shards[2], "fsdp", axis=0, tiled=True),
        lax.all_gather(shards[3], "fsdp", axis=0, tiled=True),
        lax.all_gather(shards[4], "fsdp", axis=0, tiled=True),
        lax.all_gather(shards[5], "fsdp", axis=0, tiled=True),
        lax.all_gather(shards[6], "fsdp", axis=0, tiled=True),
        lax.all_gather(shards[7], "fsdp", axis=0, tiled=True),
        lax.all_gather(shards[8], "fsdp", axis=0, tiled=True),
        lax.all_gather(shards[9], "fsdp", axis=0, tiled=True),
        lax.all_gather(shards[10], "fsdp", axis=0, tiled=True),
        lax.all_gather(shards[11], "fsdp", axis=0, tiled=True),
        lax.all_gather(shards[12], "fsdp", axis=0, tiled=True),
    )
    w_qkv = gathered[0]
    b_query = gathered[1]
    b_value = gathered[2]
    w_out = gathered[3]
    b_out = gathered[4]
    gain_one = gathered[5]
    shift_one = gathered[6]
    w_up = gathered[7]
    b_up = gathered[8]
    w_down = gathered[9]
    b_down = gathered[10]
    gain_two = gathered[11]
    shift_two = gathered[12]
    inputs = tokens[0]
    starts = doc_starts[0]
    local_count = jnp.cumsum(starts)
    offset = carried_in(local_count[-1], "seq", jnp.add, jnp.zeros((), jnp.int32))
    segment = lax.all_gather(local_count + offset, "seq", axis=0, tiled=True)
    mixed = jnp.dot(inputs, w_qkv, preferred_element_type=jnp.float32)
    query = (mixed[:, :D] + b_query).astype(jnp.bfloat16)
    key_part = mixed[:, D : 2 * D].astype(jnp.bfloat16)
    value_part = (mixed[:, 2 * D :] + b_value).astype(jnp.bfloat16)
    head_query, head_key, head_value = (
        lax.all_to_all(query, "seq", split_axis=1, concat_axis=0, tiled=True),
        lax.all_to_all(key_part, "seq", split_axis=1, concat_axis=0, tiled=True),
        lax.all_to_all(value_part, "seq", split_axis=1, concat_axis=0, tiled=True),
    )
    head_context, log_total = attend(head_query, head_key, head_value, segment)
    context = lax.all_to_all(head_context, "seq", split_axis=0, concat_axis=1, tiled=True)
    attended = jnp.dot(context, w_out, preferred_element_type=jnp.float32) + b_out
    first, normed_one, inverse_one = normalize(
        inputs.astype(jnp.float32) + attended, gain_one, shift_one
    )
    first_low = first.astype(jnp.bfloat16)
    raised = jnp.dot(first_low, w_up, preferred_element_type=jnp.float32) + b_up
    active_full, gelu_back = jax.vjp(exact_gelu, raised)
    active = active_full.astype(jnp.bfloat16)
    lowered = jnp.dot(active, w_down, preferred_element_type=jnp.float32) + b_down
    result, normed_two, inverse_two = normalize(first + lowered, gain_two, shift_two)
    again = (
        lax.all_gather(shards[0], "fsdp", axis=0, tiled=True),
        lax.all_gather(shards[1], "fsdp", axis=0, tiled=True),
        lax.all_gather(shards[2], "fsdp", axis=0, tiled=True),
        lax.all_gather(shards[3], "fsdp", axis=0, tiled=True),
        lax.all_gather(shards[4], "fsdp", axis=0, tiled=True),
        lax.all_gather(shards[5], "fsdp", axis=0, tiled=True),
        lax.all_gather(shards[6], "fsdp", axis=0, tiled=True),
        lax.all_gather(shards[7], "fsdp", axis=0, tiled=True),
        lax.all_gather(shards[8], "fsdp", axis=0, tiled=True),
        lax.all_gather(shards[9], "fsdp", axis=0, tiled=True),
        lax.all_gather(shards[10], "fsdp", axis=0, tiled=True),
        lax.all_gather(shards[11], "fsdp", axis=0, tiled=True),
        lax.all_gather(shards[12], "fsdp", axis=0, tiled=True),
    )
    w_qkv = again[0]
    w_out = again[3]
    gain_one = again[5]
    w_up = again[7]
    w_down = again[9]
    gain_two = again[11]
    upstream = cotangent[0].astype(jnp.float32)
    grad_two, d_gain_two, d_shift_two = norm_back(upstream, normed_two, inverse_two, gain_two)
    d_lowered = grad_two.astype(jnp.bfloat16)
    d_w_down = contract_rows(active, d_lowered)
    d_b_down = jnp.sum(d_lowered.astype(jnp.float32), axis=0)
    d_active = contract_cols(d_lowered, w_down)
    d_raised = gelu_back(d_active)[0].astype(jnp.bfloat16)
    d_w_up = contract_rows(first_low, d_raised)
    d_b_up = jnp.sum(d_raised.astype(jnp.float32), axis=0)
    d_first = contract_cols(d_raised, w_up) + grad_two
    grad_one, d_gain_one, d_shift_one = norm_back(d_first, normed_one, inverse_one, gain_one)
    d_attended = grad_one.astype(jnp.bfloat16)
    d_w_out = contract_rows(context, d_attended)
    d_b_out = jnp.sum(d_attended.astype(jnp.float32), axis=0)
    d_context = contract_cols(d_attended, w_out).astype(jnp.bfloat16)
    head_grad = lax.all_to_all(d_context, "seq", split_axis=1, concat_axis=0, tiled=True)
    d_query, d_key, d_value = attend_back(
        head_query, head_key, head_value, segment, log_total, head_grad
    )
    back_query, back_key, back_value = (
        lax.all_to_all(d_query, "seq", split_axis=0, concat_axis=1, tiled=True),
        lax.all_to_all(d_key, "seq", split_axis=0, concat_axis=1, tiled=True),
        lax.all_to_all(d_value, "seq", split_axis=0, concat_axis=1, tiled=True),
    )
    d_mixed = jnp.concatenate([back_query, back_key, back_value], axis=1)
    d_w_qkv = contract_rows(inputs, d_mixed)
    d_b_query = jnp.sum(back_query.astype(jnp.float32), axis=0)
    d_b_value = jnp.sum(back_value.astype(jnp.float32), axis=0)
    input_grad = grad_one + contract_cols(d_mixed, w_qkv)
    grads = (
        d_w_qkv,
        d_b_query,
        d_b_value,
        d_w_out,
        d_b_out,
        d_gain_one,
        d_shift_one,
        d_w_up,
        d_b_up,
        d_w_down,
        d_b_down,
        d_gain_two,
        d_shift_two,
    )
    owned = (
        lax.psum_scatter(grads[0], "fsdp", scatter_dimension=0, tiled=True),
        lax.psum_scatter(grads[1], "fsdp", scatter_dimension=0, tiled=True),
        lax.psum_scatter(grads[2], "fsdp", scatter_dimension=0, tiled=True),
        lax.psum_scatter(grads[3], "fsdp", scatter_dimension=0, tiled=True),
        lax.psum_scatter(grads[4], "fsdp", scatter_dimension=0, tiled=True),
        lax.psum_scatter(grads[5], "fsdp", scatter_dimension=0, tiled=True),
        lax.psum_scatter(grads[6], "fsdp", scatter_dimension=0, tiled=True),
        lax.psum_scatter(grads[7], "fsdp", scatter_dimension=0, tiled=True),
        lax.psum_scatter(grads[8], "fsdp", scatter_dimension=0, tiled=True),
        lax.psum_scatter(grads[9], "fsdp", scatter_dimension=0, tiled=True),
        lax.psum_scatter(grads[10], "fsdp", scatter_dimension=0, tiled=True),
        lax.psum_scatter(grads[11], "fsdp", scatter_dimension=0, tiled=True),
        lax.psum_scatter(grads[12], "fsdp", scatter_dimension=0, tiled=True),
    )
    totals = lax.psum(
        (
            owned[0],
            owned[1],
            owned[2],
            owned[3],
            owned[4],
            owned[5],
            owned[6],
            owned[7],
            owned[8],
            owned[9],
            owned[10],
            owned[11],
            owned[12],
        ),
        "seq",
    )
    return (
        result.astype(jnp.bfloat16)[None],
        input_grad[None],
        totals[0],
        totals[1],
        totals[2],
        totals[3],
        totals[4],
        totals[5],
        totals[6],
        totals[7],
        totals[8],
        totals[9],
        totals[10],
        totals[11],
        totals[12],
    )


def solution(mesh):
    in_specs = (
        P("fsdp", "seq", None),
        P("fsdp", "seq"),
        P("fsdp", None),
        P("fsdp"),
        P("fsdp"),
        P("fsdp", None),
        P("fsdp"),
        P("fsdp"),
        P("fsdp"),
        P("fsdp", None),
        P("fsdp"),
        P("fsdp", None),
        P("fsdp"),
        P("fsdp"),
        P("fsdp"),
        P("fsdp", "seq", None),
    )
    out_specs = (
        P("fsdp", "seq", None),
        P("fsdp", "seq", None),
        P("fsdp", None),
        P("fsdp"),
        P("fsdp"),
        P("fsdp", None),
        P("fsdp"),
        P("fsdp"),
        P("fsdp"),
        P("fsdp", None),
        P("fsdp"),
        P("fsdp", None),
        P("fsdp"),
        P("fsdp"),
        P("fsdp"),
    )
    return jax.shard_map(body, mesh=mesh, in_specs=in_specs, out_specs=out_specs, check_vma=False)
```

profile of v0, /device:TPU:0, one launch (start us, length us, event | category | flops | bytes accessed | tf_op | source)
XLA Modules:
  0.0 1540.1 jit_solution(14236879303040387469)
XLA Ops:
  9.4 22.7 %all-gather.1 = bf16[8,1,128]{2,1,0:T(2,128)(2,1)S(1)} all-gather(bf16[1,1,128]{2,1,0:T(2,128)(2,1)} %bitcast.241), channel_id=1, replica_groups=mesh['fsdp'=8,'seq'=4] {'fsdp'}, dimensions={0}, use_global_device_ids=true | all-gather | bytes 2304 | tf_op jit(solution)/shard_map/all_gather | solution.py:179
  32.1 17.2 %all-gather.2 = bf16[8,1,128]{2,1,0:T(2,128)(2,1)S(1)} all-gather(bf16[1,1,128]{2,1,0:T(2,128)(2,1)} %bitcast.242), channel_id=1, replica_groups=mesh['fsdp'=8,'seq'=4] {'fsdp'}, dimensions={0}, use_global_device_ids=true | all-gather | bytes 2304 | tf_op jit(solution)/shard_map/all_gather | solution.py:180
  49.4 62.3 %all-gather.15.cloned.1.call-done = bf16[1024,3072]{1,0:T(8,128)(2,1)} async-done(((bf16[128,3072]{1,0:T(8,128)(2,1)}), bf16[1024,3072]{1,0:T(8,128)(2,1)}) %all-gather.15.cloned.1.call-update) | async-done | bytes 6291472 | tf_op jit(solution)/shard_map/all_gather | solution.py:178
  111.7 4.9 fusion.54
  124.9 10.7 all-to-all-done
  142.0 8.7 all-to-all-done.2
  156.5 10.1 all-reduce
  170.4 5.2 all-gather
  183.6 35.5 %while.41 = (s32[]{:T(128)}, bf16[3,512,256]{2,1,0:T(8,128)(2,1)}, f32[3,4,512]{2,1,0:T(4,128)S(1)}, s32[3,512]{1,0:T(4,128)S(1)}, s32[1536]{0:T(1024)S(1)}, /*i...) while((s32[]{:T(128)}, bf16[3,512,256]{2,1,0:T(8,128)(2,1)}, ...), condition=%wide.region_7.8_spmd, body=%wide.region_4.7_spmd.sunk | while | flops 843970560 | bytes 44118632 | solution.py:91
  190.1 4.5 fusion.117
  201.9 4.5 fusion.117
  213.7 4.5 fusion.117
  223.3 18.5 %all-gather.3 = bf16[8,1,128]{2,1,0:T(2,128)(2,1)S(1)} all-gather(bf16[1,1,128]{2,1,0:T(2,128)(2,1)S(1)} %bitcast.243), channel_id=1, replica_groups=mesh['fsdp'=8,'seq'=4] {'fsdp'}, dimensions={0}, use_global_device_ids=true | all-gather | bytes 2304 | tf_op jit(solution)/shard_map/all_gather | solution.py:182
  241.9 17.3 %all-gather.4 = bf16[8,1,128]{2,1,0:T(2,128)(2,1)S(1)} all-gather(bf16[1,1,128]{2,1,0:T(2,128)(2,1)S(1)} %bitcast.244), channel_id=1, replica_groups=mesh['fsdp'=8,'seq'=4] {'fsdp'}, dimensions={0}, use_global_device_ids=true | all-gather | bytes 2304 | tf_op jit(solution)/shard_map/all_gather | solution.py:183
  259.2 18.7 %all-gather.5 = bf16[8,1,128]{2,1,0:T(2,128)(2,1)S(1)} all-gather(bf16[1,1,128]{2,1,0:T(2,128)(2,1)S(1)} %bitcast.245), channel_id=1, replica_groups=mesh['fsdp'=8,'seq'=4] {'fsdp'}, dimensions={0}, use_global_device_ids=true | all-gather | bytes 2304 | tf_op jit(solution)/shard_map/all_gather | solution.py:184
  277.9 26.8 %all-gather.6 = bf16[8,1,512]{2,1,0:T(2,128)(2,1)S(1)} all-gather(bf16[1,1,512]{2,1,0:T(2,128)(2,1)S(1)} %reshape.266), channel_id=1, replica_groups=mesh['fsdp'=8,'seq'=4] {'fsdp'}, dimensions={0}, use_global_device_ids=true | all-gather | bytes 9216 | tf_op jit(solution)/shard_map/all_gather | solution.py:186
  304.8 17.0 %all-gather.7 = bf16[8,1,128]{2,1,0:T(2,128)(2,1)S(1)} all-gather(bf16[1,1,128]{2,1,0:T(2,128)(2,1)S(1)} %bitcast.246), channel_id=1, replica_groups=mesh['fsdp'=8,'seq'=4] {'fsdp'}, dimensions={0}, use_global_device_ids=true | all-gather | bytes 2304 | tf_op jit(solution)/shard_map/all_gather | solution.py:188
  321.8 18.6 %all-gather.8 = bf16[8,1,128]{2,1,0:T(2,128)(2,1)S(1)} all-gather(bf16[1,1,128]{2,1,0:T(2,128)(2,1)S(1)} %bitcast.247), channel_id=1, replica_groups=mesh['fsdp'=8,'seq'=4] {'fsdp'}, dimensions={0}, use_global_device_ids=true | all-gather | bytes 2304 | tf_op jit(solution)/shard_map/all_gather | solution.py:189
  340.5 17.3 %all-gather.9 = bf16[8,1,128]{2,1,0:T(2,128)(2,1)S(1)} all-gather(bf16[1,1,128]{2,1,0:T(2,128)(2,1)S(1)} %bitcast.248), channel_id=1, replica_groups=mesh['fsdp'=8,'seq'=4] {'fsdp'}, dimensions={0}, use_global_device_ids=true | all-gather | bytes 2304 | tf_op jit(solution)/shard_map/all_gather | solution.py:190
  364.6 21.0 %multiply_convert_fusion.1 = (bf16[384,4096]{1,0:T(8,128)(2,1)}, f32[384,4096]{1,0:T(8,128)}, f32[384,4096]{1,0:T(8,128)}) fusion(f32[4096]{0:T(1024)S(1)} %bitcast.237, bf16[1024,4096]{1,0:T(8,128)(2,1)} %all-gather.19.cloned.1.call-done, f32[384,1024]{1,0:T(8,128)} %copy-done.7, f32[1024]{0:T(1024)S(1)} %bitcast.223, f32[1024]{0:T(1024)S(1)} %bitcast.218, ...), kind=kOutput, calls=%fused_computation.51 | convolution fusion | flops 3327000576 | bytes 25717760 | tf_op jit(solution)/shard_map/dot_general | solution.py:226
  385.6 25.7 %all-gather.21.cloned.1.call-done = bf16[4096,1024]{1,0:T(8,128)(2,1)} async-done(((bf16[512,1024]{1,0:T(8,128)(2,1)}), bf16[4096,1024]{1,0:T(8,128)(2,1)}) %all-gather.21.cloned.1.call-update) | async-done | bytes 8388624 | tf_op jit(solution)/shard_map/all_gather | solution.py:187
  411.3 8.3 fusion.73
  423.3 14.2 convert_reduce_fusion
  452.8 4.9 fusion.58
  457.6 6.7 all-to-all-done.4
  474.2 99.3 %while.42 = (s32[]{:T(128)}, f32[1536,4,64]{0,2,1:T(8,128)}, f32[1536,4,64]{0,2,1:T(8,128)}, bf16[3,512,256]{2,1,0:T(8,128)(2,1)}, bf16[3,512,4,64]{1,3,2,0:T(8,...) while((s32[]{:T(128)}, f32[1536,4,64]{0,2,1:T(8,128)}, ...), condition=%wide.region_18.19_spmd.clone, body=%wide.region_16.18_spmd.clone.sunk | while | flops 2044590080 | bytes 195090768 | solution.py:134
  477.7 5.4 multiply_reduce_fusion.7
  491.2 5.3 fusion.128
  499.5 7.2 fusion.129
  510.3 5.4 multiply_reduce_fusion.7
  523.8 5.9 fusion.128
  532.7 7.6 fusion.129
  543.8 5.4 multiply_reduce_fusion.7
  557.4 5.7 fusion.128
  566.0 7.5 fusion.129
  575.4 14.0 all_to_all.134
  596.6 7.9 all-to-all-done.5
  608.5 11.2 all-to-all-done.6
  619.6 10.9 convolution_bitcast_fusion
  631.9 10.2 fusion.67
  643.5 10.1 fusion.61
  653.8 182.3 %reduce-scatter.5.cloned.1.call-done = f32[128,3072]{0,1:T(8,128)} async-done(((f32[1024,3072]{0,1:T(8,128)}), f32[128,3072]{0,1:T(8,128)}) %reduce-scatter.5.cloned.1.call-update) | async-done | bytes 1572880 | tf_op jit(solution)/shard_map/reduce_scatter | solution.py:297
  836.1 283.0 %reduce-scatter.9.cloned.1.call-done = f32[128,4096]{1,0:T(8,128)} async-done(((f32[1024,4096]{1,0:T(8,128)}), f32[128,4096]{1,0:T(8,128)}) %reduce-scatter.9.cloned.1.call-update) | async-done | bytes 2097168 | tf_op jit(solution)/shard_map/reduce_scatter | solution.py:304
  1119.1 283.1 %reduce-scatter.11.cloned.1.call-done = f32[512,1024]{1,0:T(8,128)} async-done(((f32[4096,1024]{1,0:T(8,128)}), f32[512,1024]{1,0:T(8,128)}) %reduce-scatter.11.cloned.1.call-update) | async-done | bytes 2097168 | tf_op jit(solution)/shard_map/reduce_scatter | solution.py:306
  1404.7 35.7 %all-reduce.10 = (f32[1024]{0:T(1024)S(1)}, f32[1024]{0:T(1024)S(1)}, f32[1024]{0:T(1024)S(1)}, f32[1024]{0:T(1024)S(1)}, f32[1024]{0:T(1024)S(1)}, /*index=5*/f...) all-reduce(f32[1024]{0:T(1024)S(1)} %bitcast.236, ...), channel_id=3, replica_groups=mesh['fsdp'=8,'seq'=4] {'fsdp'}, use_global_device_ids=true, to_apply=%region_22.23.clone | all-reduce | flops 12288 | bytes 98304
  1441.1 7.5 all-reduce.11
  1448.6 7.4 add_bitcast_fusion
  1456.0 67.9 %all-reduce.15.cloned.1.call-done = (f32[128,3072]{0,1:T(8,128)}, f32[128,1024]{1,0:T(8,128)}, f32[128,4096]{1,0:T(8,128)}, f32[512,1024]{1,0:T(8,128)}) async-done(((f32[128,3072]{0,1:T(8,128)}, f32[128,1024]{1,0:T(8,128)}, f32[128,4096]{1,0:T(8,128)}, f32[512,1024]{1,0:T(8,128)}), (f32[128,3072]{0,1:T(8,128)}, f32[128,1024]{1,0:T(8,128)}, f32[128,4096]{1,0:T(8,128)}, ...) | async-done | bytes 6291472 | tf_op jit(solution)/shard_map/psum | solution.py:311
  (289 shorter events, 168.3 us)
Async XLA Ops:
  7.2 104.5 %all-gather.15.cloned.1.call-start = ((), (), s32[]{:S(2)}) async-start(), calls=%async_computation.12 | async-start | bytes 7077888 | tf_op jit(solution)/shard_map/all_gather | solution.py:178
  7.9 352.1 %all-gather.17.cloned.1.call-start = ((), (), s32[]{:S(2)}) async-start(), calls=%async_computation.13 | async-start | bytes 2359296 | tf_op jit(solution)/shard_map/all_gather | solution.py:181
  8.7 355.9 %all-gather.19.cloned.1.call-start = ((), (), s32[]{:S(2)}) async-start(), calls=%async_computation.14 | async-start | bytes 9437184 | tf_op jit(solution)/shard_map/all_gather | solution.py:185
  118.7 20.3 %copy-start.37 = (s32[1,384]{1,0:T(1,128)S(1)}, s32[1,384]{1,0:T(1,128)}, u32[]{:S(2)}) copy-start(s32[1,384]{1,0:T(1,128)} %param.23) | copy-start | bytes 4612
  120.3 34.7 %copy-start.46 = (u32[32]{0:T(128)S(1)}, u32[32]{0:T(128)}, u32[]{:S(2)}) copy-start(u32[32]{0:T(128)} %constant.152) | copy-start | bytes 388
  120.3 15.2 all-to-all-start
  135.6 15.1 all-to-all-start.2
  150.6 25.0 %copy-start.20 = (bf16[384,4,256]{2,0,1:T(8,128)(2,1)}, bf16[384,4,256]{2,0,1:T(8,128)(2,1)S(1)}, u32[]{:S(2)}) copy-start(bf16[384,4,256]{2,0,1:T(8,128)(2,1)S(1)} %all-to-all-done.2) | copy-start | bytes 2359300
  150.6 28.2 %all-to-all-start.1 = ((bf16[384,4,256]{2,0,1:T(8,128)(2,1)}), bf16[384,4,256]{2,0,1:T(8,128)(2,1)}, u32[]{:S(2)}, u32[]{:S(2)}) async-start(bf16[384,4,256]{2,0,1:T(8,128)(2,1)} %bitcast.157), calls=%async_computation.1 | async-start | bytes 1572864 | tf_op jit(solution)/shard_map/all_to_all | solution.py:216
  154.9 256.4 %all-gather.21.cloned.1.call-start = ((), (), s32[]{:S(2)}) async-start(), calls=%async_computation.15 | async-start | bytes 9437184 | tf_op jit(solution)/shard_map/all_gather | solution.py:187
  183.6 39.7 %copy-start.39 = (bf16[128]{0:T(256)(128)(2,1)S(1)}, bf16[128]{0:T(256)(128)(2,1)}, u32[]{:S(2)}) copy-start(bf16[128]{0:T(256)(128)(2,1)} %param.28) | copy-start | bytes 772
  183.6 58.3 %copy-start.40 = (bf16[128]{0:T(256)(128)(2,1)S(1)}, bf16[128]{0:T(256)(128)(2,1)}, u32[]{:S(2)}) copy-start(bf16[128]{0:T(256)(128)(2,1)} %param.29) | copy-start | bytes 772
  183.6 75.6 %copy-start.41 = (bf16[128]{0:T(256)(128)(2,1)S(1)}, bf16[128]{0:T(256)(128)(2,1)}, u32[]{:S(2)}) copy-start(bf16[128]{0:T(256)(128)(2,1)} %param.30) | copy-start | bytes 772
  183.6 94.3 %copy-start.38 = (bf16[512]{0:T(512)(128)(2,1)S(1)}, bf16[512]{0:T(512)(128)(2,1)}, u32[]{:S(2)}) copy-start(bf16[512]{0:T(512)(128)(2,1)} %param.32) | copy-start | bytes 3076
  183.6 121.2 %copy-start.42 = (bf16[128]{0:T(256)(128)(2,1)S(1)}, bf16[128]{0:T(256)(128)(2,1)}, u32[]{:S(2)}) copy-start(bf16[128]{0:T(256)(128)(2,1)} %param.34) | copy-start | bytes 772
  183.6 138.2 %copy-start.43 = (bf16[128]{0:T(256)(128)(2,1)S(1)}, bf16[128]{0:T(256)(128)(2,1)}, u32[]{:S(2)}) copy-start(bf16[128]{0:T(256)(128)(2,1)} %param.35) | copy-start | bytes 772
  183.6 156.8 %copy-start.44 = (bf16[128]{0:T(256)(128)(2,1)S(1)}, bf16[128]{0:T(256)(128)(2,1)}, u32[]{:S(2)}) copy-start(bf16[128]{0:T(256)(128)(2,1)} %param.36) | copy-start | bytes 772
  219.1 138.6 %all-to-all-start.3 = ((bf16[4,384,256]{2,1,0:T(8,128)(2,1)}), bf16[4,384,256]{2,1,0:T(8,128)(2,1)}, u32[]{:S(2)}, u32[]{:S(2)}) async-start(bf16[4,384,256]{2,1,0:T(8,128)(2,1)} %bitcast.216), calls=%async_computation.3 | async-start | bytes 1572864 | tf_op jit(solution)/shard_map/all_to_all | solution.py:220
  259.2 182.8 %copy-start.23 = (f32[8,1,128]{2,1,0:T(1,128)}, f32[8,1,128]{2,1,0:T(1,128)S(1)}, u32[]{:S(2)}) copy-start(f32[8,1,128]{2,1,0:T(1,128)S(1)} %convert_element_type.151) | copy-start | bytes 12292
  277.9 133.4 %copy-start.25 = (f32[8,1,128]{2,1,0:T(1,128)}, f32[8,1,128]{2,1,0:T(1,128)S(1)}, u32[]{:S(2)}) copy-start(f32[8,1,128]{2,1,0:T(1,128)S(1)} %convert_element_type.152) | copy-start | bytes 12292
  363.1 78.9 %copy-start.27 = (f32[384]{0:T(512)}, f32[384]{0:T(512)S(1)}, u32[]{:S(2)}) copy-start(f32[384]{0:T(512)S(1)} %broadcast_multiply_fusion.5) | copy-start | bytes 4612
  364.6 77.5 %copy-start.29 = (f32[384]{0:T(512)}, f32[384]{0:T(512)S(1)}, u32[]{:S(2)}) copy-start(f32[384]{0:T(512)S(1)} %add_rsqrt_fusion.1) | copy-start | bytes 4612
  411.3 8.6 copy-start.10
  421.2 16.4 %slice-start = ((s8[8388608]{0:T(1024)(128)(4,1)}), s8[4194304]{0:T(1024)(128)(4,1)S(1)}, s32[]{:S(2)}) async-start(s8[8388608]{0:T(1024)(128)(4,1)} %bitcast.249), calls=%async_computation.21 | async-start | bytes 8388608
  423.3 14.3 copy-start.12
  423.3 14.3 copy-start.8
  423.3 14.3 slice-start.1
  448.5 15.9 %all-to-all-start.4 = ((bf16[384,4,256]{0,2,1:T(8,128)(2,1)}), bf16[384,4,256]{0,2,1:T(8,128)(2,1)}, u32[]{:S(2)}, u32[]{:S(2)}) async-start(bf16[384,4,256]{0,2,1:T(8,128)(2,1)} %bitcast.214), calls=%async_computation.4 | async-start | bytes 1572864 | tf_op jit(solution)/shard_map/all_to_all | solution.py:267
  452.7 201.1 %reduce-scatter.7.cloned.1.call-start = ((), (), s32[]{:S(2)}) async-start(), calls=%async_computation.17 | async-start | bytes 4718592 | tf_op jit(solution)/shard_map/reduce_scatter | solution.py:300
  573.5 19.4 %copy-start.4 = (f32[1536,4,64]{0,2,1:T(8,128)S(1)}, f32[1536,4,64]{0,2,1:T(8,128)}, u32[]{:S(2)}) copy-start(f32[1536,4,64]{0,2,1:T(8,128)} %get-tuple-element.200) | copy-start | bytes 4718596
  589.4 15.1 all-to-all-start.5
  604.5 15.1 all-to-all-start.6
  608.0 228.1 %reduce-scatter.5.cloned.1.call-start = ((), (), s32[]{:S(2)}) async-start(), calls=%async_computation.16 | async-start | bytes 14155776 | tf_op jit(solution)/shard_map/reduce_scatter | solution.py:297
  608.4 22.0 %copy-start.18 = (bf16[384,4,256]{0,2,1:T(8,128)(2,1)}, bf16[384,4,256]{0,2,1:T(8,128)(2,1)S(1)}, u32[]{:S(2)}) copy-start(bf16[384,4,256]{0,2,1:T(8,128)(2,1)S(1)} %copy.95) | copy-start | bytes 2359300
  619.6 10.9 copy-start.16
  630.6 488.6 %reduce-scatter.9.cloned.1.call-start = ((), (), s32[]{:S(2)}) async-start(), calls=%async_computation.18 | async-start | bytes 18874368 | tf_op jit(solution)/shard_map/reduce_scatter | solution.py:304
  642.1 760.2 %reduce-scatter.11.cloned.1.call-start = ((), (), s32[]{:S(2)}) async-start(), calls=%async_computation.19 | async-start | bytes 18874368 | tf_op jit(solution)/shard_map/reduce_scatter | solution.py:306
  653.6 748.7 %copy-start.45 = (u32[32]{0:T(128)S(1)}, u32[32]{0:T(128)}, u32[]{:S(2)}) copy-start(u32[32]{0:T(128)} %constant.158) | copy-start | bytes 388
  653.6 750.5 %copy-start.11 = (bf16[1,384,1024]{2,1,0:T(8,128)(2,1)S(1)}, bf16[1,384,1024]{2,1,0:T(8,128)(2,1)}, u32[]{:S(2)}) copy-start(bf16[1,384,1024]{2,1,0:T(8,128)(2,1)} %param.37) | copy-start | bytes 2359300
  653.7 751.0 %copy-start.31 = (f32[1024]{0:T(1024)S(1)}, f32[1024]{0:T(1024)}, u32[]{:S(2)}) copy-start(f32[1024]{0:T(1024)} %get-tuple-element.391) | copy-start | bytes 12292
  653.7 751.0 %copy-start.32 = (f32[1024]{0:T(1024)S(1)}, f32[1024]{0:T(1024)}, u32[]{:S(2)}) copy-start(f32[1024]{0:T(1024)} %get-tuple-element.466) | copy-start | bytes 12292
  653.7 751.0 %copy-start.33 = (f32[4096]{0:T(1024)S(1)}, f32[4096]{0:T(1024)}, u32[]{:S(2)}) copy-start(f32[4096]{0:T(1024)} %get-tuple-element.483) | copy-start | bytes 49156
  653.7 751.0 %copy-start.34 = (f32[1024]{0:T(1024)S(1)}, f32[1024]{0:T(1024)}, u32[]{:S(2)}) copy-start(f32[1024]{0:T(1024)} %get-tuple-element.464) | copy-start | bytes 12292
  653.7 751.0 %copy-start.35 = (f32[1024]{0:T(1024)S(1)}, f32[1024]{0:T(1024)}, u32[]{:S(2)}) copy-start(f32[1024]{0:T(1024)} %get-tuple-element.389) | copy-start | bytes 12292
  653.7 751.0 %copy-start.36 = (f32[1024]{0:T(1024)S(1)}, f32[1024]{0:T(1024)}, u32[]{:S(2)}) copy-start(f32[1024]{0:T(1024)} %get-tuple-element.394) | copy-start | bytes 12292
  653.7 794.9 %copy-start.17 = (bf16[4,384,256]{1,2,0:T(8,128)(2,1)S(1)}, bf16[4,384,256]{1,2,0:T(8,128)(2,1)}, u32[]{:S(2)}) copy-start(bf16[4,384,256]{1,2,0:T(8,128)(2,1)} %copy-done.16) | copy-start | bytes 2359300
  653.7 870.2 %all-reduce.15.cloned.1.call-start = ((), (), s32[]{:S(2)}) async-start(), calls=%async_computation.20 | async-start | bytes 12582912 | tf_op jit(solution)/shard_map/psum | solution.py:311
  1523.9 8.2 copy-start.22
  (29 other events, 101.1 us)
Sparse Core Ops, SparseCore 0:
  10.2 101.4 all-gather.14
  113.8 47.2 all-gather.16
  163.2 123.1 all-gather.18
  288.4 122.8 all-gather.20
  457.8 87.0 reduce-scatter.6
  630.7 205.3 reduce-scatter.4
  839.9 279.1 reduce-scatter.8
  1122.9 279.3 reduce-scatter.10
  1404.8 118.9 all-reduce.14
where the time goes:
time: 1550 us; the launch traced here: 1540 us
  waiting for transfers between devices  952 us (61%)
  blocking collectives  247 us (16%)
  matrix products  192 us (12%)
  local copies, waits for them, and re-layouts  70.4 us (5%)
  other arithmetic  33.4 us (2%)
  starting transfers between devices  27.1 us (2%)
  between operations  16.1 us (1%)
    reduce_scatter x1, waiting for transfers between devices, body(): lax.psum_scatter(grads[9], 'fsdp', scatter_dimension=0, tiled=True)  283 us
    reduce_scatter x1, waiting for transfers between devices, body(): lax.psum_scatter(grads[7], 'fsdp', scatter_dimension=0, tiled=True)  283 us
    reduce_scatter x1, waiting for transfers between devices, body(): lax.psum_scatter(grads[0], 'fsdp', scatter_dimension=0, tiled=True)  182 us
    psum x1, waiting for transfers between devices, body(): lax.psum((owned[0], owned[1], owned[2], owned[3], owned[4], owned[5], own...  67.9 us
    all_gather x1, waiting for transfers between devices, body(): lax.all_gather(shards[0], 'fsdp', axis=0, tiled=True)  62.3 us
    unnamed x2, blocking collectives  45.8 us
    dot_general x4, matrix products, contract_rows(): lax.dot_general(left, right, (((0,), (0,)), ((), ())), preferred_element_...  36 us
  transfers between devices with their start and end apart: 16, of which 11 were waited for; matrix products, arithmetic and copies ran while one was open for 15% of the time, Pallas kernels for 0%

commit v1 on v0

v1 whole, which is shorter than its diff:
```python
import jax
import jax.numpy as jnp
from jax import lax
from jax.sharding import PartitionSpec as P

D = 1024
HD = 64
QBLOCK = 512


EPSILON = 1e-05


def swap(value, bit):
    count = lax.axis_size("seq")
    return lax.ppermute(value, "seq", [(place, place ^ bit) for place in range(count)])


def bits():
    count = lax.axis_size("seq")
    return [1 << power for power in reversed(range(count.bit_length() - 1))]


def gather_row(mine):
    blocks = {0: mine}
    for bit in bits():
        for place in sorted(blocks):
            blocks[place | bit] = swap(blocks[place], bit)
    return [blocks[place] for place in sorted(blocks)]


def sum_row(blocks):
    held = dict(enumerate(blocks))
    for bit in reversed(bits()):
        for place in sorted(held, reverse=True):
            if place & bit:
                term = swap(held.pop(place).astype(jnp.bfloat16), bit)
                held[place ^ bit] = held[place ^ bit] + term.astype(jnp.float32)
    return held[0]


def exchange_row(blocks):
    return [blocks[0]] + [swap(block, place) for place, block in enumerate(blocks) if place]


def in_order(blocks):
    mine, stacked = lax.axis_index("seq"), jnp.stack(blocks)
    return [lax.dynamic_index_in_dim(stacked, mine ^ place, 0, False) for place in range(len(blocks))]


def my_part(value, axis, groups=1):
    count, mine = lax.axis_size("seq"), lax.axis_index("seq")
    group = value.shape[axis] // groups
    width = group // count
    parts = [
        lax.dynamic_slice_in_dim(value, start * group + mine * width, width, axis)
        for start in range(groups)
    ]
    return parts[0] if groups == 1 else jnp.concatenate(parts, axis)


def whole_columns(pieces, groups):
    count, rows, columns = pieces.shape
    width = columns // groups
    return (
        pieces.reshape(count, rows, groups, width)
        .transpose(1, 2, 0, 3)
        .reshape(rows, groups * count * width)
    )


def split_rows(value, count):
    size = value.shape[0] // count
    return [value[place * size : (place + 1) * size] for place in range(count)]


def contract_rows(left, right):
    return lax.dot_general(
        left, right, (((0,), (0,)), ((), ())), preferred_element_type=jnp.float32
    )


def contract_cols(left, right):
    return lax.dot_general(
        left, right, (((1,), (1,)), ((), ())), preferred_element_type=jnp.float32
    )


def exact_gelu(values):
    return jax.nn.gelu(values, approximate=False)


def normalize(hidden, gain, shift):
    center = hidden - jnp.mean(hidden, axis=-1, keepdims=True)
    inverse = lax.rsqrt(jnp.mean(center * center, axis=-1, keepdims=True) + EPSILON)
    normed = center * inverse
    return (normed * gain + shift, normed, inverse)


def norm_back(incoming, normed, inverse, gain):
    scaled = incoming * gain
    d_hidden = inverse * (
        scaled
        - jnp.mean(scaled, axis=-1, keepdims=True)
        - normed * jnp.mean(scaled * normed, axis=-1, keepdims=True)
    )
    return (d_hidden, jnp.sum(incoming * normed, axis=0), jnp.sum(incoming, axis=0))


def masked_scores(query_block, segment_block, key_rows, segment, scale):
    scores = (
        jnp.einsum("qhd,khd->hqk", query_block, key_rows, preferred_element_type=jnp.float32)
        * scale
    )
    allowed = (segment_block[:, None] == segment[None, :])[None]
    return jnp.where(allowed, scores, -jnp.inf)


def attend(head_query, head_key, head_value, segment):
    length = head_query.shape[0]
    heads = head_query.shape[1] // HD
    blocks = length // QBLOCK
    scale = HD ** (-0.5)
    key_rows = head_key.reshape(length, heads, HD)
    value_rows = head_value.reshape(length, heads, HD)
    query_blocks = head_query.reshape(blocks, QBLOCK, heads, HD)
    segment_blocks = segment.reshape(blocks, QBLOCK)

    def one_block(carry, pair):
        query_block, segment_block = pair
        scores = masked_scores(query_block, segment_block, key_rows, segment, scale)
        highest = jnp.max(scores, axis=-1, keepdims=True)
        exponent = jnp.exp(scores - highest)
        total = jnp.sum(exponent, axis=-1, keepdims=True)
        weights = (exponent / total).astype(jnp.bfloat16)
        context = jnp.einsum(
            "hqk,khd->qhd", weights, value_rows, preferred_element_type=jnp.float32
        )
        context = context.astype(jnp.bfloat16).reshape(QBLOCK, heads * HD)
        return (carry, (context, (highest + jnp.log(total))[..., 0]))

    unused, (context, log_total) = lax.scan(one_block, 0, (query_blocks, segment_blocks))
    return (context.reshape(length, heads * HD), log_total)


def attend_back(head_query, head_key, head_value, segment, log_total, head_grad):
    length = head_query.shape[0]
    heads = head_query.shape[1] // HD
    blocks = length // QBLOCK
    scale = HD ** (-0.5)
    key_rows = head_key.reshape(length, heads, HD)
    value_rows = head_value.reshape(length, heads, HD)
    query_blocks = head_query.reshape(blocks, QBLOCK, heads, HD)
    grad_blocks = head_grad.reshape(blocks, QBLOCK, heads, HD)
    segment_blocks = segment.reshape(blocks, QBLOCK)

    def one_block(carry, group):
        sum_key, sum_value = carry
        query_block, segment_block, total_block, grad_block = group
        scores = masked_scores(query_block, segment_block, key_rows, segment, scale)
        probs = jnp.exp(scores - total_block[..., None])
        d_probs = jnp.einsum(
            "qhd,khd->hqk", grad_block, value_rows, preferred_element_type=jnp.float32
        )
        centre = jnp.sum(probs * d_probs, axis=-1, keepdims=True)
        d_scores = (probs * (d_probs - centre)).astype(jnp.bfloat16)
        d_query = (
            jnp.einsum("hqk,khd->qhd", d_scores, key_rows, preferred_element_type=jnp.float32)
            * scale
        )
        sum_key = (
            sum_key
            + jnp.einsum("hqk,qhd->khd", d_scores, query_block, preferred_element_type=jnp.float32)
            * scale
        )
        sum_value = sum_value + jnp.einsum(
            "hqk,qhd->khd",
            probs.astype(jnp.bfloat16),
            grad_block,
            preferred_element_type=jnp.float32,
        )
        return ((sum_key, sum_value), d_query.astype(jnp.bfloat16).reshape(QBLOCK, heads * HD))

    zeros = jnp.zeros((length, heads, HD), jnp.float32)
    (sum_key, sum_value), d_query = lax.scan(
        one_block, (zeros, zeros), (query_blocks, segment_blocks, log_total, grad_blocks)
    )
    return (
        d_query.reshape(length, heads * HD),
        sum_key.reshape(length, heads * HD).astype(jnp.bfloat16),
        sum_value.reshape(length, heads * HD).astype(jnp.bfloat16),
    )


def body(
    tokens,
    doc_starts,
    qkv_weight,
    query_bias,
    value_bias,
    out_weight,
    out_bias,
    norm1_gain,
    norm1_shift,
    up_weight,
    up_bias,
    down_weight,
    down_bias,
    norm2_gain,
    norm2_shift,
    cotangent,
):
    low = jnp.bfloat16
    seq, owners = lax.axis_size("seq"), lax.axis_size("fsdp")
    place, owner = lax.axis_index("seq"), lax.axis_index("fsdp")
    inputs = tokens[0]
    heads_width = D // seq

    w_qkv = lax.all_gather(my_part(qkv_weight, 1, 3), "fsdp", axis=0, tiled=True)
    small = jnp.concatenate(
        [
            query_bias, value_bias, out_bias, norm1_gain, norm1_shift,
            down_bias, norm2_gain, norm2_shift, up_bias,
        ]
    )
    small = lax.all_gather(small, "fsdp")
    each = D // owners
    vectors = [small[:, i * each : (i + 1) * each].reshape(D) for i in range(8)]
    b_query, b_value, b_out, gain_one, shift_one, b_down, gain_two, shift_two = vectors
    b_up = my_part(small[:, 8 * each :], 1).reshape(-1)
    my_up = my_part(up_weight, 1, owners)
    my_down = my_part(down_weight, 0)
    if my_up.shape[0] == my_down.shape[0]:
        joined = jnp.concatenate([out_weight, my_up, my_down], axis=1)
        joined = lax.all_gather(joined, "fsdp", axis=0, tiled=True)
        edge = D + my_up.shape[1]
        w_out, w_up, w_down = joined[:, :D], joined[:, D:edge], joined[:, edge:]
    else:
        w_out = lax.all_gather(out_weight, "fsdp", axis=0, tiled=True)
        w_up = lax.all_gather(my_up, "fsdp", axis=0, tiled=True)
        w_down = lax.all_gather(my_down, "fsdp", axis=0, tiled=True)
    out_rows = [
        lax.dynamic_slice_in_dim(w_out, (place ^ k) * heads_width, heads_width, 0)
        for k in range(seq)
    ]
    w_out = jnp.concatenate(out_rows, axis=0)

    row = jnp.concatenate(gather_row(inputs), axis=0)
    starts = lax.all_gather(doc_starts[0], "seq", axis=0, tiled=True)
    counts = jnp.cumsum(starts).reshape(seq, -1)
    segment = jnp.concatenate(
        [lax.dynamic_index_in_dim(counts, place ^ k, 0, False) for k in range(seq)]
    )

    mixed = jnp.dot(row, w_qkv, preferred_element_type=jnp.float32)
    query = (mixed[:, :heads_width] + my_part(b_query, 0)).astype(low)
    key_part = mixed[:, heads_width : 2 * heads_width].astype(low)
    value_part = (mixed[:, 2 * heads_width :] + my_part(b_value, 0)).astype(low)
    head_context, log_total = attend(query, key_part, value_part, segment)
    context = jnp.concatenate(exchange_row(split_rows(head_context, seq)), axis=1)
    attended = jnp.dot(context, w_out, preferred_element_type=jnp.float32) + b_out
    first, normed_one, inverse_one = normalize(
        inputs.astype(jnp.float32) + attended, gain_one, shift_one
    )
    first_row = gather_row(first.astype(low))
    raised, active, partial = [], [], []
    for block in first_row:
        lifted = jnp.dot(block, w_up, preferred_element_type=jnp.float32) + b_up
        bent = exact_gelu(lifted).astype(low)
        raised.append(lifted)
        active.append(bent)
        partial.append(jnp.dot(bent, w_down, preferred_element_type=jnp.float32))
    lowered = sum_row(partial) + b_down
    result, normed_two, inverse_two = normalize(first + lowered, gain_two, shift_two)

    upstream = cotangent[0].astype(jnp.float32)
    grad_two, d_gain_two, d_shift_two = norm_back(upstream, normed_two, inverse_two, gain_two)
    d_lowered = grad_two.astype(low)
    d_b_down = jnp.sum(d_lowered.astype(jnp.float32), axis=0)
    d_lowered_row = gather_row(d_lowered)
    d_raised, partial = [], []
    for block, lifted in zip(d_lowered_row, raised):
        d_active = contract_cols(block, w_down)
        unused, gelu_back = jax.vjp(exact_gelu, lifted)
        slope = gelu_back(d_active)[0].astype(low)
        d_raised.append(slope)
        partial.append(contract_cols(slope, w_up))
    d_first = sum_row(partial) + grad_two
    d_raised = jnp.concatenate(d_raised, axis=0)
    d_w_down = contract_rows(
        jnp.concatenate(active, axis=0), jnp.concatenate(d_lowered_row, axis=0)
    ).astype(low)
    d_w_up = contract_rows(jnp.concatenate(first_row, axis=0), d_raised).astype(low)
    d_b_up = jnp.sum(d_raised.astype(jnp.float32), axis=0)
    if my_up.shape[0] == my_down.shape[0]:
        pair = jnp.concatenate([d_w_up, d_w_down], axis=1)
        pair = lax.psum_scatter(pair, "fsdp", scatter_dimension=0, tiled=True)
        pair = lax.all_gather(pair, "seq")
        edge = d_w_up.shape[1]
        up_pieces, down_pieces = pair[:, :, :edge], pair[:, :, edge:]
    else:
        up_pieces = lax.psum_scatter(d_w_up, "fsdp", scatter_dimension=0, tiled=True)
        down_pieces = lax.psum_scatter(d_w_down, "fsdp", scatter_dimension=0, tiled=True)
        up_pieces = lax.all_gather(up_pieces, "seq")
        down_pieces = lax.all_gather(down_pieces, "seq")
    up_grad = whole_columns(up_pieces, owners).astype(jnp.float32)
    down_grad = down_pieces.reshape(-1, D).astype(jnp.float32)

    grad_one, d_gain_one, d_shift_one = norm_back(d_first, normed_one, inverse_one, gain_one)
    d_attended = grad_one.astype(low)
    d_b_out = jnp.sum(d_attended.astype(jnp.float32), axis=0)
    d_context = contract_cols(d_attended, w_out).astype(low)
    d_context = [d_context[:, k * heads_width : (k + 1) * heads_width] for k in range(seq)]
    head_grad = jnp.concatenate(exchange_row(d_context), axis=0)
    d_query, d_key, d_value = attend_back(
        query, key_part, value_part, segment, log_total, head_grad
    )
    d_mixed = jnp.concatenate([d_query, d_key, d_value], axis=1)
    d_w_qkv = contract_rows(row, d_mixed).astype(low)
    partial = [contract_cols(block, w_qkv) for block in split_rows(d_mixed, seq)]
    input_grad = grad_one + sum_row(partial)

    d_attended_row = jnp.concatenate(gather_row(d_attended), axis=0)
    d_w_out = contract_rows(head_context, d_attended_row).astype(low)
    columns = [
        lax.dynamic_slice_in_dim(d_w_out, (place ^ k) * heads_width, heads_width, 1)
        for k in range(seq)
    ]
    d_w_out = jnp.concatenate(in_order(exchange_row(columns)), axis=0)
    last = jnp.concatenate([d_w_qkv, d_w_out], axis=1)
    last = lax.psum_scatter(last, "fsdp", scatter_dimension=0, tiled=True)
    last = lax.all_gather(last, "seq")
    edge = 3 * heads_width
    qkv_grad = whole_columns(last[:, :, :edge], 3).astype(jnp.float32)
    out_grad = whole_columns(last[:, :, edge:], 1).astype(jnp.float32)

    def set_mine(part):
        whole = jnp.zeros((part.shape[0], seq, part.shape[1]), jnp.float32)
        return lax.dynamic_update_slice_in_dim(whole, part[:, None], place, 1).reshape(-1)

    d_b_query = set_mine(jnp.sum(d_query.astype(jnp.float32), axis=0)[None])
    d_b_value = set_mine(jnp.sum(d_value.astype(jnp.float32), axis=0)[None])
    d_b_up = set_mine(d_b_up.reshape(owners, -1))
    sums = (
        d_b_query, d_b_value, d_b_out, d_gain_one, d_shift_one,
        d_b_down, d_gain_two, d_shift_two, d_b_up,
    )
    totals = lax.psum(jnp.concatenate(sums), ("fsdp", "seq"))
    vectors = []
    for i, part in enumerate(sums):
        share = part.shape[0] // owners
        vectors.append(lax.dynamic_slice_in_dim(totals, i * D + owner * share, share, 0))
    return (
        result.astype(low)[None],
        input_grad[None],
        qkv_grad,
        vectors[0],
        vectors[1],
        out_grad,
        vectors[2],
        vectors[3],
        vectors[4],
        up_grad,
        vectors[8],
        down_grad,
        vectors[5],
        vectors[6],
        vectors[7],
    )


def solution(mesh):
    in_specs = (
        P("fsdp", "seq", None),
        P("fsdp", "seq"),
        P("fsdp", None),
        P("fsdp"),
        P("fsdp"),
        P("fsdp", None),
        P("fsdp"),
        P("fsdp"),
        P("fsdp"),
        P("fsdp", None),
        P("fsdp"),
        P("fsdp", None),
        P("fsdp"),
        P("fsdp"),
        P("fsdp"),
        P("fsdp", "seq", None),
    )
    out_specs = (
        P("fsdp", "seq", None),
        P("fsdp", "seq", None),
        P("fsdp", None),
        P("fsdp"),
        P("fsdp"),
        P("fsdp", None),
        P("fsdp"),
        P("fsdp"),
        P("fsdp"),
        P("fsdp", None),
        P("fsdp"),
        P("fsdp", None),
        P("fsdp"),
        P("fsdp"),
        P("fsdp"),
    )
    return jax.shard_map(body, mesh=mesh, in_specs=in_specs, out_specs=out_specs, check_vma=False)
```

time: 1550 us -> 689 us (0.44)
  waiting for transfers between devices: 952 us -> 255 us
  blocking collectives: 247 us -> 98.4 us
  other arithmetic: 33.4 us -> 62.9 us
  matrix products: 192 us -> 164 us
    reduce_scatter x4 -> x0, waiting for transfers between devices: 748 us -> none  [the longest x1 283 us: body(): lax.psum_scatter(grads[9], 'fsdp', scatter_dimension=0, tiled=True)]
    all_gather x10 -> x2, blocking collectives: 179 us -> 41.2 us  [the longest x1 31.6 us: body(): small = lax.all_gather(small, 'fsdp')]
    unnamed x9 -> x8, waiting for transfers between devices: 2.16 us -> 134 us
    ppermute x0 -> x30, waiting for transfers between devices: none -> 80.9 us  [swap(): lax.ppermute(value, 'seq', [(place, place ^ bit) for place in range(count)])]
    psum x1 -> x0, waiting for transfers between devices: 67.9 us -> none  [body(): lax.psum((owned[0], owned[1], owned[2], owned[3], owned[4], owned[5], own...]
    psum x1, blocking collectives: 7.52 us -> 57.2 us  [body(): totals = lax.psum(jnp.concatenate(sums), ('fsdp', 'seq'))]
    all_gather x4, waiting for transfers between devices: 88 us -> 39.9 us  [the longest x1 39.9 us: body(): joined = lax.all_gather(joined, 'fsdp', axis=0, tiled=True)]
    unnamed x2 -> x0, blocking collectives: 45.8 us -> none
  transfers between devices with their start and end apart: 16 -> 36, of which waited for: 11 -> 11; matrix products, arithmetic and copies ran while one was open for 15% -> 35% of each run, Pallas kernels for 0% -> 0%
where the time goes in v1:
time: 689 us; the launch traced here: 682 us
  waiting for transfers between devices  255 us (37%)
  matrix products  164 us (24%)
  blocking collectives  98.4 us (14%)
  local copies, waits for them, and re-layouts  64.6 us (9%)
  other arithmetic  62.9 us (9%)
  starting transfers between devices  20.7 us (3%)
  between operations  15.7 us (2%)
    unnamed x8, waiting for transfers between devices  134 us
    ppermute x30, waiting for transfers between devices, swap(): lax.ppermute(value, 'seq', [(place, place ^ bit) for place in range(count)])  80.9 us
    psum x1, blocking collectives, body(): totals = lax.psum(jnp.concatenate(sums), ('fsdp', 'seq'))  57.2 us
    all_gather x1, waiting for transfers between devices, body(): joined = lax.all_gather(joined, 'fsdp', axis=0, tiled=True)  39.9 us
    dot_general x4, matrix products, body(): lifted = jnp.dot(block, w_up, preferred_element_type=jnp.float32) + b_up  37.6 us
    unnamed x162, local copies, waits for them, and re-layouts  33.2 us
    all_gather x1, blocking collectives, body(): small = lax.all_gather(small, 'fsdp')  31.6 us
    dot_general x6, matrix products, masked_scores(): jnp.einsum('qhd,khd->hqk', query_block, key_rows, preferred_element_type=...  26.3 us
  transfers between devices with their start and end apart: 36, of which 11 were waited for; matrix products, arithmetic and copies ran while one was open for 35% of the time, Pallas kernels for 0%

profile of v1, /device:TPU:0, one launch (start us, length us, event | category | flops | bytes accessed | tf_op | source)
XLA Modules:
  0.0 682.5 jit_solution(13994124789272723012)
XLA Ops:
  21.2 9.6 %all-gather = s32[1,1536]{1,0:T(1,128)S(1)} all-gather(s32[1,384]{1,0:T(1,128)S(1)} %copy-done.34), channel_id=2, replica_groups=mesh['fsdp'=8,'seq'=4] {'seq'}, dimensions={1}, use_global_device_ids=true | all-gather | bytes 7680 | tf_op jit(solution)/shard_map/all_gather | solution.py:249
  33.9 31.6 %all-gather.4 = bf16[8,1,1536]{2,1,0:T(2,128)(2,1)S(1)} all-gather(bf16[1,1,1536]{2,1,0:T(2,128)(2,1)S(1)} %reshape.342), channel_id=3, replica_groups=mesh['fsdp'=8,'seq'=4] {'fsdp'}, dimensions={0}, use_global_device_ids=true | all-gather | bytes 27648 | tf_op jit(solution)/shard_map/all_gather | solution.py:226
  66.3 4.9 fusion.128
  76.4 38.5 %while.27 = (s32[]{:T(128)}, bf16[3,512,256]{2,1,0:T(8,128)(2,1)}, f32[3,4,512]{2,1,0:T(4,128)S(1)}, s32[3,512]{1,0:T(4,128)S(1)}, s32[1536]{0:T(1024)S(1)}, /*i...) while((s32[]{:T(128)}, bf16[3,512,256]{2,1,0:T(8,128)(2,1)}, ...), condition=%wide.region_5.6_spmd, body=%wide.region_2.5_spmd.sunk | while | flops 843970560 | bytes 44118132 | solution.py:142
  76.9 3.3 fusion.246
  80.3 3.5 fusion.247
  83.8 4.5 fusion.248
  89.7 3.3 fusion.246
  93.1 3.5 fusion.247
  96.6 4.5 fusion.248
  102.5 3.4 fusion.246
  105.9 3.5 fusion.247
  109.4 4.5 fusion.248
  118.1 39.9 %all-gather.12.cloned.1.call-done = bf16[1024,3072]{1,0:T(8,128)(2,1)} async-done(((bf16[128,3072]{1,0:T(8,128)(2,1)}), bf16[1024,3072]{1,0:T(8,128)(2,1)}) %all-gather.12.cloned.1.call-update) | async-done | bytes 6291472 | tf_op jit(solution)/shard_map/all_gather | solution.py:235
  165.2 16.5 %collective-permute-done.8 = bf16[384,1024]{1,0:T(8,128)(2,1)S(1)} collective-permute-done((bf16[384,1024]{1,0:T(8,128)(2,1)S(1)}, bf16[384,1024]{1,0:T(8,128)(2,1)S(1)}, u32[]{:S(2)}, u32[]{:S(2)}) %collective-permute-start.8) | collective-permute-done | bytes 786464 | tf_op jit(solution)/shard_map/ppermute | solution.py:16
  181.7 9.2 %multiply_convert_fusion.3 = (bf16[384,1024]{1,0:T(8,128)(2,1)S(1)}, f32[384,1024]{1,0:T(8,128)S(1)}, f32[384,1024]{1,0:T(8,128)S(1)}) fusion(f32[1024]{0:T(1024)S(1)} %fusion.166, bf16[384,1024]{1,0:T(8,128)(2,1)S(1)} %collective-permute-done.6, bf16[1024,3072]{1,0:T(8,128)(2,1)S(1)} %bitcast.244), kind=kOutput, calls=%fused_computation.157 | convolution fusion | flops 831258624 | bytes 6819840 | tf_op jit(solution)/shard_map/dot_general | solution.py:268
  192.6 9.7 %multiply_convert_fusion.1 = (bf16[384,1024]{1,0:T(8,128)(2,1)S(1)}, f32[384,1024]{1,0:T(8,128)S(1)}, f32[384,1024]{1,0:T(8,128)S(1)}) fusion(f32[1024]{0:T(1024)S(1)} %fusion.166, bf16[384,1024]{1,0:T(8,128)(2,1)S(1)} %collective-permute-done.9, bf16[1024,3072]{1,0:T(8,128)(2,1)S(1)} %bitcast.244), kind=kOutput, calls=%fused_computation.131 | convolution fusion | flops 831258624 | bytes 6819840 | tf_op jit(solution)/shard_map/dot_general | solution.py:268
  204.4 9.2 %multiply_convert_fusion.2 = (bf16[384,1024]{1,0:T(8,128)(2,1)S(1)}, f32[384,1024]{1,0:T(8,128)S(1)}, f32[384,1024]{1,0:T(8,128)S(1)}) fusion(f32[1024]{0:T(1024)S(1)} %fusion.166, bf16[384,1024]{1,0:T(8,128)(2,1)S(1)} %collective-permute-done.8, bf16[1024,3072]{1,0:T(8,128)(2,1)S(1)} %bitcast.244), kind=kOutput, calls=%fused_computation.144 | convolution fusion | flops 831258624 | bytes 6819840 | tf_op jit(solution)/shard_map/dot_general | solution.py:268
  217.0 9.4 %multiply_convert_fusion.4 = (bf16[384,1024]{1,0:T(8,128)(2,1)S(1)}, f32[384,1024]{1,0:T(8,128)S(1)}, f32[384,1024]{1,0:T(8,128)S(1)}) fusion(f32[1024]{0:T(1024)S(1)} %fusion.166, bf16[384,1024]{1,0:T(8,128)(2,1)S(1)} %fusion.108, bf16[1024,3072]{1,0:T(8,128)(2,1)S(1)} %bitcast.244), kind=kOutput, calls=%fused_computation.170 | convolution fusion | flops 831258624 | bytes 6819840 | tf_op jit(solution)/shard_map/dot_general | solution.py:268
  227.5 8.0 %collective-permute-done.11 = bf16[384,1024]{1,0:T(8,128)(2,1)S(1)} collective-permute-done((bf16[384,1024]{1,0:T(8,128)(2,1)S(1)}, bf16[384,1024]{1,0:T(8,128)(2,1)S(1)}, u32[]{:S(2)}, u32[]{:S(2)}) %collective-permute-start.11) | collective-permute-done | bytes 786464 | tf_op jit(solution)/shard_map/ppermute | solution.py:16
  241.2 17.6 %collective-permute-done.14 = bf16[384,1024]{1,0:T(8,128)(2,1)S(1)} collective-permute-done((bf16[384,1024]{1,0:T(8,128)(2,1)S(1)}, bf16[384,1024]{1,0:T(8,128)(2,1)S(1)}, u32[]{:S(2)}, u32[]{:S(2)}) %collective-permute-start.14) | collective-permute-done | bytes 786464 | tf_op jit(solution)/shard_map/ppermute | solution.py:16
  272.0 15.4 %collective-permute-done.17 = bf16[384,1024]{1,0:T(8,128)(2,1)S(1)} collective-permute-done((bf16[384,1024]{1,0:T(8,128)(2,1)S(1)}, bf16[384,1024]{1,0:T(8,128)(2,1)S(1)}, u32[]{:S(2)}, u32[]{:S(2)}) %collective-permute-start.17) | collective-permute-done | bytes 786464 | tf_op jit(solution)/shard_map/ppermute | solution.py:16
  287.4 3.2 multiply_reduce_fusion.1
  299.4 17.6 %collective-permute-done.20 = bf16[384,256]{1,0:T(8,128)(2,1)S(1)} collective-permute-done((bf16[384,256]{1,0:T(8,128)(2,1)}, bf16[384,256]{1,0:T(8,128)(2,1)S(1)}, u32[]{:S(2)}, u32[]{:S(2)}) %collective-permute-start.20) | collective-permute-done | bytes 196640 | tf_op jit(solution)/shard_map/ppermute | solution.py:16
  317.0 3.4 collective-permute-done.19
  324.5 3.4 copy.98
  327.9 69.3 %while.28 = (s32[]{:T(128)}, f32[1536,4,64]{0,2,1:T(8,128)}, f32[1536,4,64]{0,2,1:T(8,128)}, bf16[3,512,256]{1,2,0:T(8,128)(2,1)}, bf16[3,512,4,64]{1,3,2,0:T(8,...) while((s32[]{:T(128)}, f32[1536,4,64]{0,2,1:T(8,128)}, ...), condition=%wide.region_16.17_spmd.clone, body=%wide.region_14.16_spmd.clone.sunk | while | flops 2044590080 | bytes 137941232 | solution.py:185
  331.5 5.4 multiply_reduce_fusion.7
  337.0 3.6 multiply_convert_fusion.6
  340.5 3.5 fusion.260
  346.0 3.4 fusion.259
  353.8 5.4 multiply_reduce_fusion.7
  359.2 3.6 multiply_convert_fusion.6
  362.8 4.0 fusion.260
  368.8 3.9 fusion.259
  377.2 5.4 multiply_reduce_fusion.7
  382.6 3.6 multiply_convert_fusion.6
  386.1 4.0 fusion.260
  392.2 3.9 fusion.259
  401.6 3.4 fusion.109
  407.3 5.0 convolution_convert_fusion
  414.3 10.5 %maximum_maximum_fusion = bf16[1024,1024]{0,1:T(8,128)(2,1)S(1)} fusion(bf16[256,256]{0,1:T(8,128)(2,1)S(1)} %bitcast.259, bf16[256,256]{0,1:T(8,128)(2,1)S(1)} %bitcast.260, bf16[256,256]{0,1:T(8,128)(2,1)S(1)} %bitcast.261, bf16[256,256]{0,1:T(8,128)(2,1)S(1)} %bitcast.258, bf16[1024,768]{0,1:T(8,128)(2,1)} %convolution_convert_fusion), kind=kLoop, calls=%fused_computation.88 | loop fusion | flops 10485760 | bytes 4194304 | tf_op jit(solution)/shard_map/concatenate | solution.py:330
  427.7 6.4 fusion.70
  434.2 3.5 fusion.75
  440.1 6.5 copy.114
  446.7 48.7 %reduce-scatter.7.cloned.1.call-done = bf16[128,1024]{1,0:T(8,128)(2,1)} async-done(((bf16[1024,1024]{1,0:T(8,128)(2,1)}), bf16[128,1024]{1,0:T(8,128)(2,1)}) %reduce-scatter.7.cloned.1.call-update) | async-done | bytes 262160
  500.7 85.6 %reduce-scatter.9.cloned.1.call-done = bf16[128,2048]{1,0:T(8,128)(2,1)} async-done(((bf16[1024,2048]{1,0:T(8,128)(2,1)}), bf16[128,2048]{1,0:T(8,128)(2,1)}) %reduce-scatter.9.cloned.1.call-update) | async-done | bytes 524304
  596.7 57.2 %psum.7 = f32[12288]{0:T(1024)S(1)} all-reduce(f32[12288]{0:T(1024)S(1)} %constant_dynamic-update-slice_fusion.6), channel_id=1, replica_groups=mesh['fsdp'=8,'seq'=4] {'fsdp','seq'}, use_global_device_ids=true, to_apply=%region_27.28 | all-reduce | flops 12288 | bytes 98304 | tf_op jit(solution)/shard_map/psum | solution.py:348
  (392 shorter events, 146.8 us)
Async XLA Ops:
  7.2 59.1 %all-gather.10.cloned.1.call-start = ((), (), s32[]{:S(2)}) async-start(), calls=%async_computation.2 | async-start | bytes 1769472 | tf_op jit(solution)/shard_map/all_gather | solution.py:219
  8.2 23.7 %copy-start.39 = (bf16[128]{0:T(256)(128)(2,1)S(1)}, bf16[128]{0:T(256)(128)(2,1)}, u32[]{:S(2)}) copy-start(bf16[128]{0:T(256)(128)(2,1)} %param.27) | copy-start | bytes 772
  8.2 23.9 %copy-start.40 = (bf16[128]{0:T(256)(128)(2,1)S(1)}, bf16[128]{0:T(256)(128)(2,1)}, u32[]{:S(2)}) copy-start(bf16[128]{0:T(256)(128)(2,1)} %param.28) | copy-start | bytes 772
  8.2 24.1 %copy-start.41 = (bf16[128]{0:T(256)(128)(2,1)S(1)}, bf16[128]{0:T(256)(128)(2,1)}, u32[]{:S(2)}) copy-start(bf16[128]{0:T(256)(128)(2,1)} %param.32) | copy-start | bytes 772
  8.2 24.3 %copy-start.42 = (bf16[128]{0:T(256)(128)(2,1)S(1)}, bf16[128]{0:T(256)(128)(2,1)}, u32[]{:S(2)}) copy-start(bf16[128]{0:T(256)(128)(2,1)} %param.33) | copy-start | bytes 772
  8.3 24.5 %copy-start.43 = (bf16[128]{0:T(256)(128)(2,1)S(1)}, bf16[128]{0:T(256)(128)(2,1)}, u32[]{:S(2)}) copy-start(bf16[128]{0:T(256)(128)(2,1)} %param.34) | copy-start | bytes 772
  8.3 24.7 %copy-start.35 = (bf16[512]{0:T(512)(128)(2,1)S(1)}, bf16[512]{0:T(512)(128)(2,1)}, u32[]{:S(2)}) copy-start(bf16[512]{0:T(512)(128)(2,1)} %param.30) | copy-start | bytes 3076
  9.0 57.3 %copy-start.44 = (bf16[1,384,1024]{2,1,0:T(8,128)(2,1)S(1)}, bf16[1,384,1024]{2,1,0:T(8,128)(2,1)}, u32[]{:S(2)}) copy-start(bf16[1,384,1024]{2,1,0:T(8,128)(2,1)} %param.20) | copy-start | bytes 2359300
  9.0 149.0 %all-gather.12.cloned.1.call-start = ((), (), s32[]{:S(2)}) async-start(), calls=%async_computation.3 | async-start | bytes 7077888 | tf_op jit(solution)/shard_map/all_gather | solution.py:235
  9.1 24.0 %collective-permute-start.1 = (bf16[384,1024]{1,0:T(8,128)(2,1)}, bf16[384,1024]{1,0:T(8,128)(2,1)S(1)}, u32[]{:S(2)}, u32[]{:S(2)}) collective-permute-start(bf16[384,1024]{1,0:T(8,128)(2,1)} %bitcast.278), channel_id=1, source_target_pairs={{0,2},{1,3},{2,0},{3,1},{4,6},{5,7},{6,4},{7,5},{8,10},{9,11},{10,... | collective-permute-start | bytes 2359304 | tf_op jit(solution)/shard_map/ppermute | solution.py:16
  12.1 54.1 %collective-permute-start = (bf16[384,1024]{1,0:T(8,128)(2,1)}, bf16[384,1024]{1,0:T(8,128)(2,1)}, u32[]{:S(2)}, u32[]{:S(2)}) collective-permute-start(bf16[384,1024]{1,0:T(8,128)(2,1)} %bitcast.279), channel_id=1, source_target_pairs={{0,1},{1,0},{2,3},{3,2},{4,5},{5,4},{6,7},{7,6},{8,9},{9,8},{10,11... | collective-permute-start | bytes 2359304 | tf_op jit(solution)/shard_map/ppermute | solution.py:16
  21.1 474.3 %reduce-scatter.7.cloned.1.call-start = ((), (), s32[]{:S(2)}) async-start(), calls=%async_computation.6 | async-start | bytes 2359296
  33.0 38.1 %copy-start.47 = (bf16[384,1024]{1,0:T(8,128)(2,1)}, bf16[384,1024]{1,0:T(8,128)(2,1)S(1)}, u32[]{:S(2)}) copy-start(bf16[384,1024]{1,0:T(8,128)(2,1)S(1)} %collective-permute-done.1) | copy-start | bytes 2359300
  33.0 33.2 %collective-permute-start.2 = (bf16[384,1024]{1,0:T(8,128)(2,1)S(1)}, bf16[384,1024]{1,0:T(8,128)(2,1)S(1)}, u32[]{:S(2)}, u32[]{:S(2)}) collective-permute-start(bf16[384,1024]{1,0:T(8,128)(2,1)S(1)} %collective-permute-done.1), channel_id=1, source_target_pairs={{0,1},{1,0},{2,3},{3,2},{4,5},{5,4},{6,7},{7,6},{8,9},{9,8},{10,11... | collective-permute-start | bytes 2359304 | tf_op jit(solution)/shard_map/ppermute | solution.py:16
  116.2 43.6 %collective-permute-start.5 = (bf16[384,256]{1,0:T(8,128)(2,1)S(1)}, bf16[384,256]{1,0:T(8,128)(2,1)S(1)}, u32[]{:S(2)}, u32[]{:S(2)}) collective-permute-start(bf16[384,256]{1,0:T(8,128)(2,1)S(1)} %get-tuple-element.338), channel_id=1, source_target_pairs={{0,3},{1,2},{2,1},{3,0},{4,7},{5,6},{6,5},{7,4},{8,11},{9,10},{10,... | collective-permute-start | bytes 589832 | tf_op jit(solution)/shard_map/ppermute | solution.py:16
  116.2 43.5 %collective-permute-start.4 = (bf16[384,256]{1,0:T(8,128)(2,1)S(1)}, bf16[384,256]{1,0:T(8,128)(2,1)}, u32[]{:S(2)}, u32[]{:S(2)}) collective-permute-start(bf16[384,256]{1,0:T(8,128)(2,1)S(1)} %get-tuple-element.339), channel_id=1, source_target_pairs={{0,2},{1,3},{2,0},{3,1},{4,6},{5,7},{6,4},{7,5},{8,10},{9,11},{10,... | collective-permute-start | bytes 589832 | tf_op jit(solution)/shard_map/ppermute | solution.py:16
  117.9 41.9 %collective-permute-start.3 = (bf16[384,256]{1,0:T(8,128)(2,1)S(1)}, bf16[384,256]{1,0:T(8,128)(2,1)}, u32[]{:S(2)}, u32[]{:S(2)}) collective-permute-start(bf16[384,256]{1,0:T(8,128)(2,1)S(1)} %get-tuple-element.340), channel_id=1, source_target_pairs={{0,1},{1,0},{2,3},{3,2},{4,5},{5,4},{6,7},{7,6},{8,9},{9,8},{10,11... | collective-permute-start | bytes 589832 | tf_op jit(solution)/shard_map/ppermute | solution.py:16
  163.6 53.4 %copy-start.17 = (bf16[384,1024]{1,0:T(8,128)(2,1)}, bf16[384,1024]{1,0:T(8,128)(2,1)S(1)}, u32[]{:S(2)}) copy-start(bf16[384,1024]{1,0:T(8,128)(2,1)S(1)} %fusion.108) | copy-start | bytes 2359300
  163.6 18.0 %collective-permute-start.8 = (bf16[384,1024]{1,0:T(8,128)(2,1)S(1)}, bf16[384,1024]{1,0:T(8,128)(2,1)S(1)}, u32[]{:S(2)}, u32[]{:S(2)}) collective-permute-start(bf16[384,1024]{1,0:T(8,128)(2,1)S(1)} %fusion.108), channel_id=1, source_target_pairs={{0,2},{1,3},{2,0},{3,1},{4,6},{5,7},{6,4},{7,5},{8,10},{9,11},{10,... | collective-permute-start | bytes 2359304 | tf_op jit(solution)/shard_map/ppermute | solution.py:16
  165.2 16.5 %collective-permute-start.6 = (bf16[384,1024]{1,0:T(8,128)(2,1)S(1)}, bf16[384,1024]{1,0:T(8,128)(2,1)S(1)}, u32[]{:S(2)}, u32[]{:S(2)}) collective-permute-start(bf16[384,1024]{1,0:T(8,128)(2,1)S(1)} %fusion.108), channel_id=1, source_target_pairs={{0,1},{1,0},{2,3},{3,2},{4,5},{5,4},{6,7},{7,6},{8,9},{9,8},{10,11... | collective-permute-start | bytes 2359304 | tf_op jit(solution)/shard_map/ppermute | solution.py:16
  181.7 10.9 %collective-permute-start.9 = (bf16[384,1024]{1,0:T(8,128)(2,1)S(1)}, bf16[384,1024]{1,0:T(8,128)(2,1)S(1)}, u32[]{:S(2)}, u32[]{:S(2)}) collective-permute-start(bf16[384,1024]{1,0:T(8,128)(2,1)S(1)} %collective-permute-done.8), channel_id=1, source_target_pairs={{0,1},{1,0},{2,3},{3,2},{4,5},{5,4},{6,7},{7,6},{8,9},{9,8},{10,11... | collective-permute-start | bytes 2359304 | tf_op jit(solution)/shard_map/ppermute | solution.py:16
  192.0 35.5 %collective-permute-start.7 = (bf16[384,1024]{1,0:T(8,128)(2,1)S(1)}, bf16[384,1024]{1,0:T(8,128)(2,1)S(1)}, u32[]{:S(2)}, u32[]{:S(2)}) collective-permute-start(bf16[384,1024]{1,0:T(8,128)(2,1)S(1)} %convolution_convert_fusion.7), channel_id=1, source_target_pairs={{0,1},{1,0},{2,3},{3,2},{4,5},{5,4},{6,7},{7,6},{8,9},{9,8},{10,11... | collective-permute-start | bytes 2359304 | tf_op jit(solution)/shard_map/ppermute | solution.py:16
  204.3 9.4 %collective-permute-start.10 = (bf16[384,1024]{1,0:T(8,128)(2,1)S(1)}, bf16[384,1024]{1,0:T(8,128)(2,1)S(1)}, u32[]{:S(2)}, u32[]{:S(2)}) collective-permute-start(bf16[384,1024]{1,0:T(8,128)(2,1)S(1)} %convolution_convert_fusion.6), channel_id=1, source_target_pairs={{0,1},{1,0},{2,3},{3,2},{4,5},{5,4},{6,7},{7,6},{8,9},{9,8},{10,11... | collective-permute-start | bytes 2359304 | tf_op jit(solution)/shard_map/ppermute | solution.py:16
  215.5 20.0 %collective-permute-start.11 = (bf16[384,1024]{1,0:T(8,128)(2,1)S(1)}, bf16[384,1024]{1,0:T(8,128)(2,1)S(1)}, u32[]{:S(2)}, u32[]{:S(2)}) collective-permute-start(bf16[384,1024]{1,0:T(8,128)(2,1)S(1)} %add_convert_fusion.7), channel_id=1, source_target_pairs={{0,2},{1,3},{2,0},{3,1},{4,6},{5,7},{6,4},{7,5},{8,10},{9,11},{10,... | collective-permute-start | bytes 2359304 | tf_op jit(solution)/shard_map/ppermute | solution.py:16
  239.8 29.5 %copy-start.23 = (bf16[384,1024]{1,0:T(8,128)(2,1)}, bf16[384,1024]{1,0:T(8,128)(2,1)S(1)}, u32[]{:S(2)}) copy-start(bf16[384,1024]{1,0:T(8,128)(2,1)S(1)} %get-tuple-element.303) | copy-start | bytes 2359300
  239.8 19.0 %collective-permute-start.14 = (bf16[384,1024]{1,0:T(8,128)(2,1)S(1)}, bf16[384,1024]{1,0:T(8,128)(2,1)S(1)}, u32[]{:S(2)}, u32[]{:S(2)}) collective-permute-start(bf16[384,1024]{1,0:T(8,128)(2,1)S(1)} %get-tuple-element.303), channel_id=1, source_target_pairs={{0,2},{1,3},{2,0},{3,1},{4,6},{5,7},{6,4},{7,5},{8,10},{9,11},{10,... | collective-permute-start | bytes 2359304 | tf_op jit(solution)/shard_map/ppermute | solution.py:16
  241.2 17.6 %collective-permute-start.12 = (bf16[384,1024]{1,0:T(8,128)(2,1)S(1)}, bf16[384,1024]{1,0:T(8,128)(2,1)S(1)}, u32[]{:S(2)}, u32[]{:S(2)}) collective-permute-start(bf16[384,1024]{1,0:T(8,128)(2,1)S(1)} %get-tuple-element.303), channel_id=1, source_target_pairs={{0,1},{1,0},{2,3},{3,2},{4,5},{5,4},{6,7},{7,6},{8,9},{9,8},{10,11... | collective-permute-start | bytes 2359304 | tf_op jit(solution)/shard_map/ppermute | solution.py:16
  258.8 2.3 collective-permute-start.15
  263.6 3.1 collective-permute-start.16
  264.8 7.1 %collective-permute-start.13 = (bf16[384,1024]{1,0:T(8,128)(2,1)S(1)}, bf16[384,1024]{1,0:T(8,128)(2,1)S(1)}, u32[]{:S(2)}, u32[]{:S(2)}) collective-permute-start(bf16[384,1024]{1,0:T(8,128)(2,1)S(1)} %convolution_convert_fusion.5), channel_id=1, source_target_pairs={{0,1},{1,0},{2,3},{3,2},{4,5},{5,4},{6,7},{7,6},{8,9},{9,8},{10,11... | collective-permute-start | bytes 2359304 | tf_op jit(solution)/shard_map/ppermute | solution.py:16
  267.8 19.6 %collective-permute-start.17 = (bf16[384,1024]{1,0:T(8,128)(2,1)S(1)}, bf16[384,1024]{1,0:T(8,128)(2,1)S(1)}, u32[]{:S(2)}, u32[]{:S(2)}) collective-permute-start(bf16[384,1024]{1,0:T(8,128)(2,1)S(1)} %add_convert_fusion.1), channel_id=1, source_target_pairs={{0,2},{1,3},{2,0},{3,1},{4,6},{5,7},{6,4},{7,5},{8,10},{9,11},{10,... | collective-permute-start | bytes 2359304 | tf_op jit(solution)/shard_map/ppermute | solution.py:16
  293.1 34.7 %collective-permute-start.25 = (bf16[384,1024]{1,0:T(8,128)(2,1)}, bf16[384,1024]{1,0:T(8,128)(2,1)}, u32[]{:S(2)}, u32[]{:S(2)}) collective-permute-start(bf16[384,1024]{1,0:T(8,128)(2,1)} %get-tuple-element.305), channel_id=1, source_target_pairs={{0,2},{1,3},{2,0},{3,1},{4,6},{5,7},{6,4},{7,5},{8,10},{9,11},{10,... | collective-permute-start | bytes 2359304 | tf_op jit(solution)/shard_map/ppermute | solution.py:16
  297.5 19.5 %collective-permute-start.20 = (bf16[384,256]{1,0:T(8,128)(2,1)}, bf16[384,256]{1,0:T(8,128)(2,1)S(1)}, u32[]{:S(2)}, u32[]{:S(2)}) collective-permute-start(bf16[384,256]{1,0:T(8,128)(2,1)} %get-tuple-element.334), channel_id=1, source_target_pairs={{0,3},{1,2},{2,1},{3,0},{4,7},{5,6},{6,5},{7,4},{8,11},{9,10},{10,... | collective-permute-start | bytes 589832 | tf_op jit(solution)/shard_map/ppermute | solution.py:16
  297.5 22.9 %collective-permute-start.19 = (bf16[384,256]{1,0:T(8,128)(2,1)S(1)}, bf16[384,256]{1,0:T(8,128)(2,1)S(1)}, u32[]{:S(2)}, u32[]{:S(2)}) collective-permute-start(bf16[384,256]{1,0:T(8,128)(2,1)S(1)} %get-tuple-element.335), channel_id=1, source_target_pairs={{0,2},{1,3},{2,0},{3,1},{4,6},{5,7},{6,4},{7,5},{8,10},{9,11},{10,... | collective-permute-start | bytes 589832 | tf_op jit(solution)/shard_map/ppermute | solution.py:16
  298.2 22.3 %collective-permute-start.18 = (bf16[384,256]{1,0:T(8,128)(2,1)S(1)}, bf16[384,256]{1,0:T(8,128)(2,1)S(1)}, u32[]{:S(2)}, u32[]{:S(2)}) collective-permute-start(bf16[384,256]{1,0:T(8,128)(2,1)S(1)} %get-tuple-element.336), channel_id=1, source_target_pairs={{0,1},{1,0},{2,3},{3,2},{4,5},{5,4},{6,7},{7,6},{8,9},{9,8},{10,11... | collective-permute-start | bytes 589832 | tf_op jit(solution)/shard_map/ppermute | solution.py:16
  299.4 102.2 %collective-permute-start.24 = (bf16[384,1024]{1,0:T(8,128)(2,1)}, bf16[384,1024]{1,0:T(8,128)(2,1)}, u32[]{:S(2)}, u32[]{:S(2)}) collective-permute-start(bf16[384,1024]{1,0:T(8,128)(2,1)} %get-tuple-element.305), channel_id=1, source_target_pairs={{0,1},{1,0},{2,3},{3,2},{4,5},{5,4},{6,7},{7,6},{8,9},{9,8},{10,11... | collective-permute-start | bytes 2359304 | tf_op jit(solution)/shard_map/ppermute | solution.py:16
  327.9 73.7 %collective-permute-start.26 = (bf16[384,1024]{1,0:T(8,128)(2,1)}, bf16[384,1024]{1,0:T(8,128)(2,1)}, u32[]{:S(2)}, u32[]{:S(2)}) collective-permute-start(bf16[384,1024]{1,0:T(8,128)(2,1)} %collective-permute-done.25), channel_id=1, source_target_pairs={{0,1},{1,0},{2,3},{3,2},{4,5},{5,4},{6,7},{7,6},{8,9},{9,8},{10,11... | collective-permute-start | bytes 2359304 | tf_op jit(solution)/shard_map/ppermute | solution.py:16
  405.1 7.2 %collective-permute-start.29 = (bf16[256,256]{1,0:T(8,128)(2,1)S(1)}, bf16[256,256]{1,0:T(8,128)(2,1)S(1)}, u32[]{:S(2)}, u32[]{:S(2)}) collective-permute-start(bf16[256,256]{1,0:T(8,128)(2,1)S(1)} %get-tuple-element.349), channel_id=1, source_target_pairs={{0,3},{1,2},{2,1},{3,0},{4,7},{5,6},{6,5},{7,4},{8,11},{9,10},{10,... | collective-permute-start | bytes 393224 | tf_op jit(solution)/shard_map/ppermute | solution.py:16
  406.7 7.0 %collective-permute-start.28 = (bf16[256,256]{1,0:T(8,128)(2,1)S(1)}, bf16[256,256]{1,0:T(8,128)(2,1)S(1)}, u32[]{:S(2)}, u32[]{:S(2)}) collective-permute-start(bf16[256,256]{1,0:T(8,128)(2,1)S(1)} %get-tuple-element.350), channel_id=1, source_target_pairs={{0,2},{1,3},{2,0},{3,1},{4,6},{5,7},{6,4},{7,5},{8,10},{9,11},{10,... | collective-permute-start | bytes 393224 | tf_op jit(solution)/shard_map/ppermute | solution.py:16
  407.3 6.5 collective-permute-start.27
  427.4 158.9 %reduce-scatter.9.cloned.1.call-start = ((), (), s32[]{:S(2)}) async-start(), calls=%async_computation.7 | async-start | bytes 4718592
  446.6 50.7 %copy-start.4 = (bf16[1,384,1024]{2,1,0:T(8,128)(2,1)S(1)}, bf16[1,384,1024]{2,1,0:T(8,128)(2,1)}, u32[]{:S(2)}) copy-start(bf16[1,384,1024]{2,1,0:T(8,128)(2,1)} %param.35) | copy-start | bytes 2359300
  446.6 213.8 %all-gather.14.cloned.1.call-start = ((), (), s32[]{:S(2)}) async-start(), calls=%async_computation.4 | async-start | bytes 1310720 | tf_op jit(solution)/shard_map/all_gather | solution.py:332
  497.2 169.5 %all-gather.16.cloned.1.call-start = ((), (), s32[]{:S(2)}) async-start(), calls=%async_computation.5 | async-start | bytes 2621440 | tf_op jit(solution)/shard_map/all_gather | solution.py:298
  500.7 87.7 %copy-start.10 = (bf16[3,512,256]{1,2,0:T(8,128)(2,1)S(1)}, bf16[3,512,256]{1,2,0:T(8,128)(2,1)}, u32[]{:S(2)}) copy-start(bf16[3,512,256]{1,2,0:T(8,128)(2,1)} %get-tuple-element.119) | copy-start | bytes 2359300
  591.2 2.4 collective-permute-start.22
  592.9 64.6 %collective-permute-start.21 = (bf16[384,1024]{1,0:T(8,128)(2,1)}, bf16[384,1024]{1,0:T(8,128)(2,1)S(1)}, u32[]{:S(2)}, u32[]{:S(2)}) collective-permute-start(bf16[384,1024]{1,0:T(8,128)(2,1)} %convolution_convert_fusion.2), channel_id=1, source_target_pairs={{0,1},{1,0},{2,3},{3,2},{4,5},{5,4},{6,7},{7,6},{8,9},{9,8},{10,11... | collective-permute-start | bytes 2359304 | tf_op jit(solution)/shard_map/ppermute | solution.py:16
  595.2 62.4 %collective-permute-start.23 = (bf16[384,1024]{1,0:T(8,128)(2,1)}, bf16[384,1024]{1,0:T(8,128)(2,1)}, u32[]{:S(2)}, u32[]{:S(2)}) collective-permute-start(bf16[384,1024]{1,0:T(8,128)(2,1)} %add_convert_fusion), channel_id=1, source_target_pairs={{0,2},{1,3},{2,0},{3,1},{4,6},{5,7},{6,4},{7,5},{8,10},{9,11},{10,... | collective-permute-start | bytes 2359304 | tf_op jit(solution)/shard_map/ppermute | solution.py:16
  (62 other events, 359.1 us)
Sparse Core Ops, SparseCore 0:
  10.7 47.2 all-gather.9
  60.8 97.1 all-gather.11
  427.5 67.8 reduce-scatter.6
  498.9 87.3 reduce-scatter.8
  588.3 21.7 all-gather.13
  612.1 23.4 all-gather.15

commit v2 on v1

--- a/solution.py
+++ b/solution.py
@@ -86,8 +86,15 @@
     )
 
 
-def exact_gelu(values):
-    return jax.nn.gelu(values, approximate=False)
+def gelu_and_slope(values):
+    phi = 0.5 + 0.5 * lax.erf(values * (0.5**0.5))
+    density = jnp.exp(-0.5 * values * values) * ((2.0 * jnp.pi) ** -0.5)
+    return values * phi, phi + values * density
+
+
+def as_columns(vectors, rows):
+    padded = [jnp.pad(vector, (0, rows - vector.shape[0])) for vector in vectors]
+    return jnp.pad(jnp.stack(padded, axis=1), ((0, 0), (0, -len(vectors) % 128)))
 
 
 def normalize(hidden, gain, shift):
@@ -212,22 +219,26 @@
 ):
     low = jnp.bfloat16
     seq, owners = lax.axis_size("seq"), lax.axis_size("fsdp")
-    place, owner = lax.axis_index("seq"), lax.axis_index("fsdp")
+    place = lax.axis_index("seq")
     inputs = tokens[0]
     heads_width = D // seq
 
-    w_qkv = lax.all_gather(my_part(qkv_weight, 1, 3), "fsdp", axis=0, tiled=True)
-    small = jnp.concatenate(
+    each = D // owners
+    columns = as_columns(
         [
             query_bias, value_bias, out_bias, norm1_gain, norm1_shift,
-            down_bias, norm2_gain, norm2_shift, up_bias,
-        ]
-    )
-    small = lax.all_gather(small, "fsdp")
-    each = D // owners
-    vectors = [small[:, i * each : (i + 1) * each].reshape(D) for i in range(8)]
-    b_query, b_value, b_out, gain_one, shift_one, b_down, gain_two, shift_two = vectors
-    b_up = my_part(small[:, 8 * each :], 1).reshape(-1)
+            down_bias, norm2_gain, norm2_shift, my_part(up_bias, 0),
+        ],
+        each,
+    )
+    w_qkv = jnp.concatenate([my_part(qkv_weight, 1, 3), columns], axis=1)
+    w_qkv = lax.all_gather(w_qkv, "fsdp", axis=0, tiled=True)
+    small = w_qkv[:, 3 * heads_width :].T
+    w_qkv = w_qkv[:, : 3 * heads_width]
+    b_query, b_value, b_out, gain_one, shift_one, b_down, gain_two, shift_two = [
+        small[i] for i in range(8)
+    ]
+    b_up = small[8].reshape(owners, each)[:, : up_bias.shape[0] // seq].reshape(-1)
     my_up = my_part(up_weight, 1, owners)
     my_down = my_part(down_weight, 0)
     if my_up.shape[0] == my_down.shape[0]:
@@ -246,11 +257,11 @@
     w_out = jnp.concatenate(out_rows, axis=0)
 
     row = jnp.concatenate(gather_row(inputs), axis=0)
-    starts = lax.all_gather(doc_starts[0], "seq", axis=0, tiled=True)
-    counts = jnp.cumsum(starts).reshape(seq, -1)
-    segment = jnp.concatenate(
-        [lax.dynamic_index_in_dim(counts, place ^ k, 0, False) for k in range(seq)]
-    )
+    counts = jnp.cumsum(jnp.stack(gather_row(doc_starts[0])), axis=1)
+    spots = place ^ jnp.arange(seq)
+    before = (spots[None, :] < spots[:, None]).astype(jnp.int32)
+    counts = counts + jnp.sum(before * counts[:, -1][None, :], axis=1)[:, None]
+    segment = counts.reshape(-1)
 
     mixed = jnp.dot(row, w_qkv, preferred_element_type=jnp.float32)
     query = (mixed[:, :heads_width] + my_part(b_query, 0)).astype(low)
@@ -263,11 +274,12 @@
         inputs.astype(jnp.float32) + attended, gain_one, shift_one
     )
     first_row = gather_row(first.astype(low))
-    raised, active, partial = [], [], []
+    slopes, active, partial = [], [], []
     for block in first_row:
-        lifted = jnp.dot(block, w_up, preferred_element_type=jnp.float32) + b_up
-        bent = exact_gelu(lifted).astype(low)
-        raised.append(lifted)
+        raised = jnp.dot(block, w_up, preferred_element_type=jnp.float32) + b_up
+        bent, slope = gelu_and_slope(raised)
+        bent = bent.astype(low)
+        slopes.append(slope)
         active.append(bent)
         partial.append(jnp.dot(bent, w_down, preferred_element_type=jnp.float32))
     lowered = sum_row(partial) + b_down
@@ -279,12 +291,10 @@
     d_b_down = jnp.sum(d_lowered.astype(jnp.float32), axis=0)
     d_lowered_row = gather_row(d_lowered)
     d_raised, partial = [], []
-    for block, lifted in zip(d_lowered_row, raised):
-        d_active = contract_cols(block, w_down)
-        unused, gelu_back = jax.vjp(exact_gelu, lifted)
-        slope = gelu_back(d_active)[0].astype(low)
-        d_raised.append(slope)
-        partial.append(contract_cols(slope, w_up))
+    for block, slope in zip(d_lowered_row, slopes):
+        turned = (contract_cols(block, w_down) * slope).astype(low)
+        d_raised.append(turned)
+        partial.append(contract_cols(turned, w_up))
     d_first = sum_row(partial) + grad_two
     d_raised = jnp.concatenate(d_raised, axis=0)
     d_w_down = contract_rows(
@@ -292,19 +302,6 @@
     ).astype(low)
     d_w_up = contract_rows(jnp.concatenate(first_row, axis=0), d_raised).astype(low)
     d_b_up = jnp.sum(d_raised.astype(jnp.float32), axis=0)
-    if my_up.shape[0] == my_down.shape[0]:
-        pair = jnp.concatenate([d_w_up, d_w_down], axis=1)
-        pair = lax.psum_scatter(pair, "fsdp", scatter_dimension=0, tiled=True)
-        pair = lax.all_gather(pair, "seq")
-        edge = d_w_up.shape[1]
-        up_pieces, down_pieces = pair[:, :, :edge], pair[:, :, edge:]
-    else:
-        up_pieces = lax.psum_scatter(d_w_up, "fsdp", scatter_dimension=0, tiled=True)
-        down_pieces = lax.psum_scatter(d_w_down, "fsdp", scatter_dimension=0, tiled=True)
-        up_pieces = lax.all_gather(up_pieces, "seq")
-        down_pieces = lax.all_gather(down_pieces, "seq")
-    up_grad = whole_columns(up_pieces, owners).astype(jnp.float32)
-    down_grad = down_pieces.reshape(-1, D).astype(jnp.float32)
 
     grad_one, d_gain_one, d_shift_one = norm_back(d_first, normed_one, inverse_one, gain_one)
     d_attended = grad_one.astype(low)
@@ -312,6 +309,31 @@
     d_context = contract_cols(d_attended, w_out).astype(low)
     d_context = [d_context[:, k * heads_width : (k + 1) * heads_width] for k in range(seq)]
     head_grad = jnp.concatenate(exchange_row(d_context), axis=0)
+    d_b_up = d_b_up.reshape(owners, -1)
+    d_b_up = jnp.pad(d_b_up, ((0, 0), (0, each - d_b_up.shape[1]))).reshape(-1)
+    columns = as_columns(
+        [d_b_out, d_gain_one, d_shift_one, d_b_down, d_gain_two, d_shift_two, d_b_up], D
+    ).astype(low)
+    if my_up.shape[0] == my_down.shape[0]:
+        pair = jnp.concatenate([d_w_up, d_w_down, columns], axis=1)
+        head_grad, pair = lax.optimization_barrier((head_grad, pair))
+        pair = lax.psum_scatter(pair, "fsdp", scatter_dimension=0, tiled=True)
+        pair = lax.all_gather(pair, "seq")
+        edge = d_w_up.shape[1]
+        up_pieces, down_pieces = pair[:, :, :edge], pair[:, :, edge : edge + D]
+        column_pieces = pair[:, :, edge + D :]
+    else:
+        up_pieces = jnp.concatenate([d_w_up, columns], axis=1)
+        up_pieces = lax.psum_scatter(up_pieces, "fsdp", scatter_dimension=0, tiled=True)
+        down_pieces = lax.psum_scatter(d_w_down, "fsdp", scatter_dimension=0, tiled=True)
+        up_pieces = lax.all_gather(up_pieces, "seq")
+        down_pieces = lax.all_gather(down_pieces, "seq")
+        edge = d_w_up.shape[1]
+        up_pieces, column_pieces = up_pieces[:, :, :edge], up_pieces[:, :, edge:]
+    up_grad = whole_columns(up_pieces, owners).astype(jnp.float32)
+    down_grad = down_pieces.reshape(-1, D).astype(jnp.float32)
+    small_grads = jnp.sum(column_pieces.astype(jnp.float32), axis=0).T
+    up_bias_grad = column_pieces[:, : up_bias.shape[0] // seq, 6].reshape(-1).astype(jnp.float32)
     d_query, d_key, d_value = attend_back(
         query, key_part, value_part, segment, log_total, head_grad
     )
@@ -327,45 +349,36 @@
         for k in range(seq)
     ]
     d_w_out = jnp.concatenate(in_order(exchange_row(columns)), axis=0)
-    last = jnp.concatenate([d_w_qkv, d_w_out], axis=1)
+
+    def set_mine(part):
+        whole = jnp.zeros((D,), jnp.float32)
+        part = jnp.sum(part.astype(jnp.float32), axis=0)
+        return lax.dynamic_update_slice_in_dim(whole, part, place * heads_width, 0)
+
+    columns = as_columns([set_mine(d_query), set_mine(d_value)], D).astype(low)
+    last = jnp.concatenate([d_w_qkv, d_w_out, columns], axis=1)
     last = lax.psum_scatter(last, "fsdp", scatter_dimension=0, tiled=True)
     last = lax.all_gather(last, "seq")
     edge = 3 * heads_width
     qkv_grad = whole_columns(last[:, :, :edge], 3).astype(jnp.float32)
-    out_grad = whole_columns(last[:, :, edge:], 1).astype(jnp.float32)
-
-    def set_mine(part):
-        whole = jnp.zeros((part.shape[0], seq, part.shape[1]), jnp.float32)
-        return lax.dynamic_update_slice_in_dim(whole, part[:, None], place, 1).reshape(-1)
-
-    d_b_query = set_mine(jnp.sum(d_query.astype(jnp.float32), axis=0)[None])
-    d_b_value = set_mine(jnp.sum(d_value.astype(jnp.float32), axis=0)[None])
-    d_b_up = set_mine(d_b_up.reshape(owners, -1))
-    sums = (
-        d_b_query, d_b_value, d_b_out, d_gain_one, d_shift_one,
-        d_b_down, d_gain_two, d_shift_two, d_b_up,
-    )
-    totals = lax.psum(jnp.concatenate(sums), ("fsdp", "seq"))
-    vectors = []
-    for i, part in enumerate(sums):
-        share = part.shape[0] // owners
-        vectors.append(lax.dynamic_slice_in_dim(totals, i * D + owner * share, share, 0))
+    out_grad = whole_columns(last[:, :, edge : edge + heads_width], 1).astype(jnp.float32)
+    late_grads = jnp.sum(last[:, :, edge + heads_width :].astype(jnp.float32), axis=0).T
     return (
         result.astype(low)[None],
         input_grad[None],
         qkv_grad,
-        vectors[0],
-        vectors[1],
+        late_grads[0],
+        late_grads[1],
         out_grad,
-        vectors[2],
-        vectors[3],
-        vectors[4],
+        small_grads[0],
+        small_grads[1],
+        small_grads[2],
         up_grad,
-        vectors[8],
+        up_bias_grad,
         down_grad,
-        vectors[5],
-        vectors[6],
-        vectors[7],
+        small_grads[3],
+        small_grads[4],
+        small_grads[5],
     )
 
 

time: 689 us -> 726 us (1.054)
  waiting for transfers between devices: 255 us -> 354 us
  blocking collectives: 98.4 us -> 0 us
  local copies, waits for them, and re-layouts: 64.6 us -> 85.2 us
  matrix products: 164 us -> 174 us
  other arithmetic: 62.9 us -> 70.5 us
    psum x1 -> x0, blocking collectives: 57.2 us -> none  [body(): totals = lax.psum(jnp.concatenate(sums), ('fsdp', 'seq'))]
    all_gather x2 -> x0, blocking collectives: 41.2 us -> none  [the longest x1 31.6 us: body(): small = lax.all_gather(small, 'fsdp')]
    ppermute x30 -> x33, waiting for transfers between devices: 80.9 us -> 116 us  [swap(): lax.ppermute(value, 'seq', [(place, place ^ bit) for place in range(count)])]
    dot_general x4, matrix products: 37.6 us -> 10 us  [body(): raised = jnp.dot(block, w_up, preferred_element_type=jnp.float32) + b_up]
    all_gather x1, waiting for transfers between devices: 0.02 us -> 24.8 us  [body(): w_qkv = lax.all_gather(w_qkv, 'fsdp', axis=0, tiled=True)]
    unnamed x8, waiting for transfers between devices: 134 us -> 155 us
    dot_general x3, matrix products: 8.31 us -> 22.2 us  [one_block(): jnp.einsum('qhd,khd->hqk', grad_block, value_rows, preferred_element_type...]
    while x18 -> x54, local copies, waits for them, and re-layouts: 1.03 us -> 13.7 us
  transfers between devices with their start and end apart: 36 -> 39, of which waited for: 11 -> 18; matrix products, arithmetic and copies ran while one was open for 35% -> 35% of each run, Pallas kernels for 0% -> 0%
where the time goes in v2:
time: 726 us; the launch traced here: 723 us
  waiting for transfers between devices  354 us (49%)
  matrix products  174 us (24%)
  local copies, waits for them, and re-layouts  85.2 us (12%)
  other arithmetic  70.5 us (10%)
  starting transfers between devices  23.1 us (3%)
  between operations  15.4 us (2%)
    unnamed x8, waiting for transfers between devices  155 us
    ppermute x33, waiting for transfers between devices, swap(): lax.ppermute(value, 'seq', [(place, place ^ bit) for place in range(count)])  116 us
    all_gather x1, waiting for transfers between devices, body(): joined = lax.all_gather(joined, 'fsdp', axis=0, tiled=True)  49.8 us
    unnamed x118, local copies, waits for them, and re-layouts  33.1 us
    dot_general x6, matrix products, masked_scores(): jnp.einsum('qhd,khd->hqk', query_block, key_rows, preferred_element_type=...  30.4 us
    all_gather x1, waiting for transfers between devices, body(): w_qkv = lax.all_gather(w_qkv, 'fsdp', axis=0, tiled=True)  24.8 us
    ppermute x33, starting transfers between devices, swap(): lax.ppermute(value, 'seq', [(place, place ^ bit) for place in range(count)])  22.9 us
    dot_general x3, matrix products, one_block(): jnp.einsum('qhd,khd->hqk', grad_block, value_rows, preferred_element_type...  22.2 us
  transfers between devices with their start and end apart: 39, of which 18 were waited for; matrix products, arithmetic and copies ran while one was open for 35% of the time, Pallas kernels for 0%

profile of v2, /device:TPU:0, one launch (start us, length us, event | category | flops | bytes accessed | tf_op | source)
XLA Modules:
  0.0 723.1 jit_solution(12991673894345726016)
XLA Ops:
  24.2 7.3 %collective-permute-done.1 = s32[384]{0:T(512)S(1)} collective-permute-done((s32[384]{0:T(512)S(1)}, s32[384]{0:T(512)S(1)}, u32[]{:S(2)}, u32[]{:S(2)}) %collective-permute-start.1) | collective-permute-done | bytes 1568 | tf_op jit(solution)/shard_map/ppermute | solution.py:16
  35.2 24.8 %all-gather.7.cloned.1.call-done = bf16[1024,896]{1,0:T(8,128)(2,1)} async-done(((bf16[128,896]{1,0:T(8,128)(2,1)}), bf16[1024,896]{1,0:T(8,128)(2,1)}) %all-gather.7.cloned.1.call-update) | async-done | bytes 1835024 | tf_op jit(solution)/shard_map/all_gather | solution.py:235
  61.1 4.8 fusion.127
  69.2 36.1 %while.27 = (s32[]{:T(128)}, bf16[3,512,256]{2,1,0:T(8,128)(2,1)}, f32[3,4,512]{2,1,0:T(4,128)S(1)}, s32[3,512]{1,0:T(4,128)S(1)}, s32[4,384]{1,0:T(4,128)S(1)},...) while((s32[]{:T(128)}, bf16[3,512,256]{2,1,0:T(8,128)(2,1)}, ...), condition=%wide.region_6.7_spmd, body=%wide.region_3.6_spmd.sunk | while | flops 843970560 | bytes 44130920 | solution.py:149
  72.2 3.5 fusion.240
  75.7 4.6 fusion.241
  87.6 4.6 fusion.241
  96.0 3.5 fusion.240
  99.6 4.6 fusion.241
  110.3 49.8 %all-gather.9.cloned.1.call-done = bf16[1024,3072]{1,0:T(8,128)(2,1)} async-done(((bf16[128,3072]{1,0:T(8,128)(2,1)}), bf16[1024,3072]{1,0:T(8,128)(2,1)}) %all-gather.9.cloned.1.call-update) | async-done | bytes 6291472 | tf_op jit(solution)/shard_map/all_gather | solution.py:246
  168.2 16.5 %collective-permute-done.11 = bf16[384,1024]{1,0:T(8,128)(2,1)S(1)} collective-permute-done((bf16[384,1024]{1,0:T(8,128)(2,1)S(1)}, bf16[384,1024]{1,0:T(8,128)(2,1)S(1)}, u32[]{:S(2)}, u32[]{:S(2)}) %collective-permute-start.11) | collective-permute-done | bytes 786464 | tf_op jit(solution)/shard_map/ppermute | solution.py:16
  209.1 11.0 %collective-permute-done.14 = bf16[384,1024]{1,0:T(8,128)(2,1)} collective-permute-done((bf16[384,1024]{1,0:T(8,128)(2,1)}, bf16[384,1024]{1,0:T(8,128)(2,1)}, u32[]{:S(2)}, u32[]{:S(2)}) %collective-permute-start.14) | collective-permute-done | bytes 786464 | tf_op jit(solution)/shard_map/ppermute | solution.py:16
  224.1 12.8 %fusion.180 = (bf16[1024]{0:T(1024)(128)(2,1)S(1)}, bf16[384,1024]{1,0:T(8,128)(2,1)S(1)}) fusion(f32[384]{0:T(512)S(1)} %broadcast_multiply_fusion.2, f32[384,1024]{1,0:T(8,128)S(1)} %get-tuple-element.400, f32[384]{0:T(512)S(1)} %broadcast_multiply_fusion.4, f32[384]{0:T(512)S(1)} %broadcast_multiply_fusion.3, f32[1024]{0:T(1024)S(1)} %get-tuple-element.340, ...), kind=kLoop, calls=%fused_computation.304 | loop fusion | flops 3931136 | bytes 3158016 | tf_op jit(solution)/shard_map/reduce_sum | solution.py:291
  241.3 15.7 %collective-permute-done.17 = bf16[384,1024]{1,0:T(8,128)(2,1)S(1)} collective-permute-done((bf16[384,1024]{1,0:T(8,128)(2,1)S(1)}, bf16[384,1024]{1,0:T(8,128)(2,1)S(1)}, u32[]{:S(2)}, u32[]{:S(2)}) %collective-permute-start.17) | collective-permute-done | bytes 786464 | tf_op jit(solution)/shard_map/ppermute | solution.py:16
  267.8 6.5 fusion.82
  278.2 4.9 fusion.77
  283.1 13.4 %collective-permute-done.20 = bf16[384,1024]{1,0:T(8,128)(2,1)S(1)} collective-permute-done((bf16[384,1024]{1,0:T(8,128)(2,1)S(1)}, bf16[384,1024]{1,0:T(8,128)(2,1)S(1)}, u32[]{:S(2)}, u32[]{:S(2)}) %collective-permute-start.20) | collective-permute-done | bytes 786464 | tf_op jit(solution)/shard_map/ppermute | solution.py:16
  307.8 3.8 fusion.35
  311.6 17.0 %collective-permute-done.22 = bf16[384,256]{1,0:T(8,128)(2,1)} collective-permute-done((bf16[384,256]{1,0:T(8,128)(2,1)S(1)}, bf16[384,256]{1,0:T(8,128)(2,1)}, u32[]{:S(2)}, u32[]{:S(2)}) %collective-permute-start.22) | collective-permute-done | bytes 196640 | tf_op jit(solution)/shard_map/ppermute | solution.py:16
  339.1 118.4 %while.28 = (s32[]{:T(128)}, f32[1536,4,64]{0,2,1:T(8,128)}, f32[1536,4,64]{0,2,1:T(8,128)}, bf16[3,512,256]{1,2,0:T(8,128)(2,1)}, bf16[3,512,4,64]{1,3,2,0:T(8,...) while((s32[]{:T(128)}, f32[1536,4,64]{0,2,1:T(8,128)}, ...), condition=%wide.region_24.25_spmd.clone, body=%wide.region_22.24_spmd.clone.sunk | while | flops 2044590080 | bytes 257493392 | solution.py:192
  339.1 7.4 %fusion.251 = f32[4,512,1536]{2,1,0:T(8,128)} fusion(bf16[1536,4,64]{0,2,1:T(8,128)(2,1)S(1)} %get-tuple-element.644, bf16[3,512,4,64]{1,3,2,0:T(8,128)(2,1)} %get-tuple-element.643, s32[]{:T(128)} %get-tuple-element.621), kind=kOutput, calls=%fused_computation.32.clone.1 | convolution fusion | flops 402653184 | bytes 13632000 | tf_op jit(solution)/shard_map/while/body/eval_jaxpr/qhd,khd->hqk/dot_general | solution.py:169
  347.1 7.7 %multiply_reduce_fusion.7 = (f32[4,512]{1,0:T(4,128)S(1)}, f32[4,512,1536]{2,1,0:T(8,128)S(1)}) fusion(f32[4,512,1536]{2,1,0:T(8,128)} %fusion.251, f32[4,512]{1,0:T(4,128)S(1)} %dynamic-slice_bitcast_fusion.4, bf16[1536,4,64]{0,2,1:T(8,128)(2,1)S(1)} %get-tuple-element.641, bf16[3,512,4,64]{1,3,2,0:T(8,128)(2,1)} %copy-done.9, ...), kind=kOutput, calls=%fused_computation.18.clone.1 | convolution fusion | flops 418379776 | bytes 27017728 | tf_op jit(solution)/shard_map/while/body/eval_jaxpr/qhd,khd->hqk/dot_general | solution.py:119
  354.8 4.5 copy-done.2
  359.4 3.6 multiply_convert_fusion.6
  362.9 5.3 fusion.252
  368.3 5.4 fusion.254
  377.8 7.4 %fusion.251 = f32[4,512,1536]{2,1,0:T(8,128)} fusion(bf16[1536,4,64]{0,2,1:T(8,128)(2,1)S(1)} %get-tuple-element.644, bf16[3,512,4,64]{1,3,2,0:T(8,128)(2,1)} %get-tuple-element.643, s32[]{:T(128)} %get-tuple-element.621), kind=kOutput, calls=%fused_computation.32.clone.1 | convolution fusion | flops 402653184 | bytes 13632000 | tf_op jit(solution)/shard_map/while/body/eval_jaxpr/qhd,khd->hqk/dot_general | solution.py:169
  385.8 7.7 %multiply_reduce_fusion.7 = (f32[4,512]{1,0:T(4,128)S(1)}, f32[4,512,1536]{2,1,0:T(8,128)S(1)}) fusion(f32[4,512,1536]{2,1,0:T(8,128)} %fusion.251, f32[4,512]{1,0:T(4,128)S(1)} %dynamic-slice_bitcast_fusion.4, bf16[1536,4,64]{0,2,1:T(8,128)(2,1)S(1)} %get-tuple-element.641, bf16[3,512,4,64]{1,3,2,0:T(8,128)(2,1)} %copy-done.9, ...), kind=kOutput, calls=%fused_computation.18.clone.1 | convolution fusion | flops 418379776 | bytes 27017728 | tf_op jit(solution)/shard_map/while/body/eval_jaxpr/qhd,khd->hqk/dot_general | solution.py:119
  393.6 4.5 copy-done.2
  398.1 3.6 multiply_convert_fusion.6
  401.7 5.8 fusion.252
  407.5 5.4 fusion.254
  413.6 4.0 fusion.253
  417.6 7.4 %fusion.251 = f32[4,512,1536]{2,1,0:T(8,128)} fusion(bf16[1536,4,64]{0,2,1:T(8,128)(2,1)S(1)} %get-tuple-element.644, bf16[3,512,4,64]{1,3,2,0:T(8,128)(2,1)} %get-tuple-element.643, s32[]{:T(128)} %get-tuple-element.621), kind=kOutput, calls=%fused_computation.32.clone.1 | convolution fusion | flops 402653184 | bytes 13632000 | tf_op jit(solution)/shard_map/while/body/eval_jaxpr/qhd,khd->hqk/dot_general | solution.py:169
  425.6 7.7 %multiply_reduce_fusion.7 = (f32[4,512]{1,0:T(4,128)S(1)}, f32[4,512,1536]{2,1,0:T(8,128)S(1)}) fusion(f32[4,512,1536]{2,1,0:T(8,128)} %fusion.251, f32[4,512]{1,0:T(4,128)S(1)} %dynamic-slice_bitcast_fusion.4, bf16[1536,4,64]{0,2,1:T(8,128)(2,1)S(1)} %get-tuple-element.641, bf16[3,512,4,64]{1,3,2,0:T(8,128)(2,1)} %copy-done.9, ...), kind=kOutput, calls=%fused_computation.18.clone.1 | convolution fusion | flops 418379776 | bytes 27017728 | tf_op jit(solution)/shard_map/while/body/eval_jaxpr/qhd,khd->hqk/dot_general | solution.py:119
  433.3 4.5 copy-done.2
  437.9 3.6 multiply_convert_fusion.6
  441.4 5.8 fusion.252
  447.2 5.4 fusion.254
  453.4 4.0 fusion.253
  463.5 5.8 convolution_convert_fusion
  474.0 4.5 collective-permute-done.31
  482.7 5.6 pad_maximum_fusion.2
  491.0 6.6 copy.183
  497.7 62.5 %reduce-scatter.7.cloned.1.call-done = bf16[128,1152]{1,0:T(8,128)(2,1)} async-done(((bf16[1024,1152]{1,0:T(8,128)(2,1)}), bf16[128,1152]{1,0:T(8,128)(2,1)}) %reduce-scatter.7.cloned.1.call-update) | async-done | bytes 294928
  562.1 92.9 %reduce-scatter.9.cloned.1.call-done = bf16[128,2176]{1,0:T(8,128)(2,1)} async-done(((bf16[1024,2176]{1,0:T(8,128)(2,1)}), bf16[128,2176]{1,0:T(8,128)(2,1)}) %reduce-scatter.9.cloned.1.call-update) | async-done | bytes 557072
  665.0 23.6 %collective-permute-done.26 = bf16[384,1024]{1,0:T(8,128)(2,1)S(1)} collective-permute-done((bf16[384,1024]{1,0:T(8,128)(2,1)S(1)}, bf16[384,1024]{1,0:T(8,128)(2,1)S(1)}, u32[]{:S(2)}, u32[]{:S(2)}) %collective-permute-start.26) | collective-permute-done | bytes 786464 | tf_op jit(solution)/shard_map/ppermute | solution.py:16
  697.8 7.8 %all-gather.13.cloned.1.call-done = bf16[512,2176]{0,1:T(8,128)(2,1)} async-done(((bf16[128,2176]{0,1:T(8,128)(2,1)}), bf16[512,2176]{0,1:T(8,128)(2,1)}) %all-gather.13.cloned.1.call-update) | async-done | bytes 2228240 | tf_op jit(solution)/shard_map/all_gather | solution.py:321
  (408 shorter events, 177.9 us)
Async XLA Ops:
  7.2 52.7 %all-gather.7.cloned.1.call-start = ((), (), s32[]{:S(2)}) async-start(), calls=%async_computation.2 | async-start | bytes 2064384 | tf_op jit(solution)/shard_map/all_gather | solution.py:235
  10.6 149.6 %all-gather.9.cloned.1.call-start = ((), (), s32[]{:S(2)}) async-start(), calls=%async_computation.3 | async-start | bytes 7077888 | tf_op jit(solution)/shard_map/all_gather | solution.py:246
  10.6 24.0 %collective-permute-start.4 = (bf16[384,1024]{1,0:T(8,128)(2,1)}, bf16[384,1024]{1,0:T(8,128)(2,1)S(1)}, u32[]{:S(2)}, u32[]{:S(2)}) collective-permute-start(bf16[384,1024]{1,0:T(8,128)(2,1)} %bitcast.254), channel_id=1, source_target_pairs={{0,2},{1,3},{2,0},{3,1},{4,6},{5,7},{6,4},{7,5},{8,10},{9,11},{10,... | collective-permute-start | bytes 2359304 | tf_op jit(solution)/shard_map/ppermute | solution.py:16
  13.7 47.4 %collective-permute-start.3 = (bf16[384,1024]{1,0:T(8,128)(2,1)}, bf16[384,1024]{1,0:T(8,128)(2,1)}, u32[]{:S(2)}, u32[]{:S(2)}) collective-permute-start(bf16[384,1024]{1,0:T(8,128)(2,1)} %bitcast.255), channel_id=1, source_target_pairs={{0,1},{1,0},{2,3},{3,2},{4,5},{5,4},{6,7},{7,6},{8,9},{9,8},{10,11... | collective-permute-start | bytes 2359304 | tf_op jit(solution)/shard_map/ppermute | solution.py:16
  14.4 17.1 %collective-permute-start.1 = (s32[384]{0:T(512)S(1)}, s32[384]{0:T(512)S(1)}, u32[]{:S(2)}, u32[]{:S(2)}) collective-permute-start(s32[384]{0:T(512)S(1)} %reduce.11), channel_id=1, source_target_pairs={{0,2},{1,3},{2,0},{3,1},{4,6},{5,7},{6,4},{7,5},{8,10},{9,11},{10,... | collective-permute-start | bytes 4616 | tf_op jit(solution)/shard_map/ppermute | solution.py:16
  14.5 17.0 %collective-permute-start = (s32[384]{0:T(512)S(1)}, s32[384]{0:T(512)S(1)}, u32[]{:S(2)}, u32[]{:S(2)}) collective-permute-start(s32[384]{0:T(512)S(1)} %reduce.11), channel_id=1, source_target_pairs={{0,1},{1,0},{2,3},{3,2},{4,5},{5,4},{6,7},{7,6},{8,9},{9,8},{10,11... | collective-permute-start | bytes 4616 | tf_op jit(solution)/shard_map/ppermute | solution.py:16
  15.0 46.0 %copy-start.29 = (bf16[1,384,1024]{2,1,0:T(8,128)(2,1)S(1)}, bf16[1,384,1024]{2,1,0:T(8,128)(2,1)}, u32[]{:S(2)}) copy-start(bf16[1,384,1024]{2,1,0:T(8,128)(2,1)} %param.20) | copy-start | bytes 2359300
  24.1 536.0 %reduce-scatter.7.cloned.1.call-start = ((), (), s32[]{:S(2)}) async-start(), calls=%async_computation.6 | async-start | bytes 2654208
  31.5 1.2 collective-permute-start.2
  34.6 26.5 %copy-start.31 = (bf16[384,1024]{1,0:T(8,128)(2,1)}, bf16[384,1024]{1,0:T(8,128)(2,1)S(1)}, u32[]{:S(2)}) copy-start(bf16[384,1024]{1,0:T(8,128)(2,1)S(1)} %collective-permute-done.4) | copy-start | bytes 2359300
  34.6 26.5 %collective-permute-start.5 = (bf16[384,1024]{1,0:T(8,128)(2,1)S(1)}, bf16[384,1024]{1,0:T(8,128)(2,1)S(1)}, u32[]{:S(2)}, u32[]{:S(2)}) collective-permute-start(bf16[384,1024]{1,0:T(8,128)(2,1)S(1)} %collective-permute-done.4), channel_id=1, source_target_pairs={{0,1},{1,0},{2,3},{3,2},{4,5},{5,4},{6,7},{7,6},{8,9},{9,8},{10,11... | collective-permute-start | bytes 2359304 | tf_op jit(solution)/shard_map/ppermute | solution.py:16
  107.3 54.6 %collective-permute-start.6 = (bf16[384,256]{1,0:T(8,128)(2,1)}, bf16[384,256]{1,0:T(8,128)(2,1)}, u32[]{:S(2)}, u32[]{:S(2)}) collective-permute-start(bf16[384,256]{1,0:T(8,128)(2,1)} %get-tuple-element.421), channel_id=1, source_target_pairs={{0,1},{1,0},{2,3},{3,2},{4,5},{5,4},{6,7},{7,6},{8,9},{9,8},{10,11... | collective-permute-start | bytes 589832 | tf_op jit(solution)/shard_map/ppermute | solution.py:16
  107.3 54.6 %collective-permute-start.7 = (bf16[384,256]{1,0:T(8,128)(2,1)}, bf16[384,256]{1,0:T(8,128)(2,1)}, u32[]{:S(2)}, u32[]{:S(2)}) collective-permute-start(bf16[384,256]{1,0:T(8,128)(2,1)} %get-tuple-element.420), channel_id=1, source_target_pairs={{0,2},{1,3},{2,0},{3,1},{4,6},{5,7},{6,4},{7,5},{8,10},{9,11},{10,... | collective-permute-start | bytes 589832 | tf_op jit(solution)/shard_map/ppermute | solution.py:16
  108.8 53.2 %collective-permute-start.8 = (bf16[384,256]{1,0:T(8,128)(2,1)S(1)}, bf16[384,256]{1,0:T(8,128)(2,1)}, u32[]{:S(2)}, u32[]{:S(2)}) collective-permute-start(bf16[384,256]{1,0:T(8,128)(2,1)S(1)} %get-tuple-element.419), channel_id=1, source_target_pairs={{0,3},{1,2},{2,1},{3,0},{4,7},{5,6},{6,5},{7,4},{8,11},{9,10},{10,... | collective-permute-start | bytes 589832 | tf_op jit(solution)/shard_map/ppermute | solution.py:16
  161.9 25.0 %slice-start.3 = ((s8[6291456]{0:T(1024)(128)(4,1)}), s8[4194304]{0:T(1024)(128)(4,1)S(1)}, s32[]{:S(2)}) async-start(s8[6291456]{0:T(1024)(128)(4,1)} %bitcast.210), calls=%async_computation.11 | async-start | bytes 8388608
  162.9 24.0 %slice-start.4 = ((s8[6291456]{0:T(1024)(128)(4,1)}), s8[2097152]{0:T(1024)(128)(4,1)S(1)}, s32[]{:S(2)}) async-start(s8[6291456]{0:T(1024)(128)(4,1)} %bitcast.210), calls=%async_computation.12 | async-start | bytes 4194304
  166.7 18.0 %collective-permute-start.11 = (bf16[384,1024]{1,0:T(8,128)(2,1)S(1)}, bf16[384,1024]{1,0:T(8,128)(2,1)S(1)}, u32[]{:S(2)}, u32[]{:S(2)}) collective-permute-start(bf16[384,1024]{1,0:T(8,128)(2,1)S(1)} %fusion.117), channel_id=1, source_target_pairs={{0,2},{1,3},{2,0},{3,1},{4,6},{5,7},{6,4},{7,5},{8,10},{9,11},{10,... | collective-permute-start | bytes 2359304 | tf_op jit(solution)/shard_map/ppermute | solution.py:16
  184.7 2.3 collective-permute-start.12
  184.7 6.8 collective-permute-start.9
  191.2 7.1 collective-permute-start.13
  195.6 13.5 %collective-permute-start.10 = (bf16[384,1024]{1,0:T(8,128)(2,1)}, bf16[384,1024]{1,0:T(8,128)(2,1)}, u32[]{:S(2)}, u32[]{:S(2)}) collective-permute-start(bf16[384,1024]{1,0:T(8,128)(2,1)} %convolution_convert_fusion.7), channel_id=1, source_target_pairs={{0,1},{1,0},{2,3},{3,2},{4,5},{5,4},{6,7},{7,6},{8,9},{9,8},{10,11... | collective-permute-start | bytes 2359304 | tf_op jit(solution)/shard_map/ppermute | solution.py:16
  200.2 19.9 %collective-permute-start.14 = (bf16[384,1024]{1,0:T(8,128)(2,1)}, bf16[384,1024]{1,0:T(8,128)(2,1)}, u32[]{:S(2)}, u32[]{:S(2)}) collective-permute-start(bf16[384,1024]{1,0:T(8,128)(2,1)} %add_convert_fusion.3), channel_id=1, source_target_pairs={{0,2},{1,3},{2,0},{3,1},{4,6},{5,7},{6,4},{7,5},{8,10},{9,11},{10,... | collective-permute-start | bytes 2359304 | tf_op jit(solution)/shard_map/ppermute | solution.py:16
  203.0 35.6 %slice-start.5 = ((s8[6291456]{0:T(1024)(128)(4,1)}), s8[4194304]{0:T(1024)(128)(4,1)S(1)}, s32[]{:S(2)}) async-start(s8[6291456]{0:T(1024)(128)(4,1)} %bitcast.212), calls=%async_computation.13 | async-start | bytes 8388608
  206.2 32.5 %slice-start.6 = ((s8[6291456]{0:T(1024)(128)(4,1)}), s8[2097152]{0:T(1024)(128)(4,1)S(1)}, s32[]{:S(2)}) async-start(s8[6291456]{0:T(1024)(128)(4,1)} %bitcast.212), calls=%async_computation.14 | async-start | bytes 4194304
  237.0 20.0 %collective-permute-start.15 = (bf16[384,1024]{1,0:T(8,128)(2,1)S(1)}, bf16[384,1024]{1,0:T(8,128)(2,1)S(1)}, u32[]{:S(2)}, u32[]{:S(2)}) collective-permute-start(bf16[384,1024]{1,0:T(8,128)(2,1)S(1)} %get-tuple-element.394), channel_id=1, source_target_pairs={{0,1},{1,0},{2,3},{3,2},{4,5},{5,4},{6,7},{7,6},{8,9},{9,8},{10,11... | collective-permute-start | bytes 2359304 | tf_op jit(solution)/shard_map/ppermute | solution.py:16
  237.0 19.9 %collective-permute-start.17 = (bf16[384,1024]{1,0:T(8,128)(2,1)S(1)}, bf16[384,1024]{1,0:T(8,128)(2,1)S(1)}, u32[]{:S(2)}, u32[]{:S(2)}) collective-permute-start(bf16[384,1024]{1,0:T(8,128)(2,1)S(1)} %get-tuple-element.394), channel_id=1, source_target_pairs={{0,2},{1,3},{2,0},{3,1},{4,6},{5,7},{6,4},{7,5},{8,10},{9,11},{10,... | collective-permute-start | bytes 2359304 | tf_op jit(solution)/shard_map/ppermute | solution.py:16
  257.0 6.5 collective-permute-start.18
  260.6 22.6 %collective-permute-start.16 = (bf16[384,1024]{1,0:T(8,128)(2,1)S(1)}, bf16[384,1024]{1,0:T(8,128)(2,1)S(1)}, u32[]{:S(2)}, u32[]{:S(2)}) collective-permute-start(bf16[384,1024]{1,0:T(8,128)(2,1)S(1)} %convolution_convert_fusion.5), channel_id=1, source_target_pairs={{0,1},{1,0},{2,3},{3,2},{4,5},{5,4},{6,7},{7,6},{8,9},{9,8},{10,11... | collective-permute-start | bytes 2359304 | tf_op jit(solution)/shard_map/ppermute | solution.py:16
  267.0 7.3 %collective-permute-start.19 = (bf16[384,1024]{1,0:T(8,128)(2,1)S(1)}, bf16[384,1024]{1,0:T(8,128)(2,1)S(1)}, u32[]{:S(2)}, u32[]{:S(2)}) collective-permute-start(bf16[384,1024]{1,0:T(8,128)(2,1)S(1)} %convolution_convert_fusion.4), channel_id=1, source_target_pairs={{0,1},{1,0},{2,3},{3,2},{4,5},{5,4},{6,7},{7,6},{8,9},{9,8},{10,11... | collective-permute-start | bytes 2359304 | tf_op jit(solution)/shard_map/ppermute | solution.py:16
  276.6 19.8 %collective-permute-start.20 = (bf16[384,1024]{1,0:T(8,128)(2,1)S(1)}, bf16[384,1024]{1,0:T(8,128)(2,1)S(1)}, u32[]{:S(2)}, u32[]{:S(2)}) collective-permute-start(bf16[384,1024]{1,0:T(8,128)(2,1)S(1)} %add_convert_fusion.1), channel_id=1, source_target_pairs={{0,2},{1,3},{2,0},{3,1},{4,6},{5,7},{6,4},{7,5},{8,10},{9,11},{10,... | collective-permute-start | bytes 2359304 | tf_op jit(solution)/shard_map/ppermute | solution.py:16
  303.2 159.1 %collective-permute-start.28 = (bf16[384,1024]{1,0:T(8,128)(2,1)}, bf16[384,1024]{1,0:T(8,128)(2,1)}, u32[]{:S(2)}, u32[]{:S(2)}) collective-permute-start(bf16[384,1024]{1,0:T(8,128)(2,1)} %get-tuple-element.396), channel_id=1, source_target_pairs={{0,2},{1,3},{2,0},{3,1},{4,6},{5,7},{6,4},{7,5},{8,10},{9,11},{10,... | collective-permute-start | bytes 2359304 | tf_op jit(solution)/shard_map/ppermute | solution.py:16
  305.1 164.1 %collective-permute-start.27 = (bf16[384,1024]{1,0:T(8,128)(2,1)}, bf16[384,1024]{1,0:T(8,128)(2,1)}, u32[]{:S(2)}, u32[]{:S(2)}) collective-permute-start(bf16[384,1024]{1,0:T(8,128)(2,1)} %get-tuple-element.396), channel_id=1, source_target_pairs={{0,1},{1,0},{2,3},{3,2},{4,5},{5,4},{6,7},{7,6},{8,9},{9,8},{10,11... | collective-permute-start | bytes 2359304 | tf_op jit(solution)/shard_map/ppermute | solution.py:16
  305.9 5.7 collective-permute-start.21
  306.4 22.2 %collective-permute-start.22 = (bf16[384,256]{1,0:T(8,128)(2,1)S(1)}, bf16[384,256]{1,0:T(8,128)(2,1)}, u32[]{:S(2)}, u32[]{:S(2)}) collective-permute-start(bf16[384,256]{1,0:T(8,128)(2,1)S(1)} %get-tuple-element.416), channel_id=1, source_target_pairs={{0,2},{1,3},{2,0},{3,1},{4,6},{5,7},{6,4},{7,5},{8,10},{9,11},{10,... | collective-permute-start | bytes 589832 | tf_op jit(solution)/shard_map/ppermute | solution.py:16
  307.0 23.2 %collective-permute-start.23 = (bf16[384,256]{1,0:T(8,128)(2,1)S(1)}, bf16[384,256]{1,0:T(8,128)(2,1)}, u32[]{:S(2)}, u32[]{:S(2)}) collective-permute-start(bf16[384,256]{1,0:T(8,128)(2,1)S(1)} %get-tuple-element.415), channel_id=1, source_target_pairs={{0,3},{1,2},{2,1},{3,0},{4,7},{5,6},{6,5},{7,4},{8,11},{9,10},{10,... | collective-permute-start | bytes 589832 | tf_op jit(solution)/shard_map/ppermute | solution.py:16
  462.3 7.0 collective-permute-start.29
  472.0 2.0 collective-permute-start.30
  472.1 6.4 collective-permute-start.31
  473.6 6.6 collective-permute-start.32
  490.9 164.1 %reduce-scatter.9.cloned.1.call-start = ((), (), s32[]{:S(2)}) async-start(), calls=%async_computation.7 | async-start | bytes 5013504
  497.6 159.5 %copy-start.14 = (bf16[1536,256]{1,0:T(8,128)(2,1)S(1)}, bf16[1536,256]{1,0:T(8,128)(2,1)}, u32[]{:S(2)}) copy-start(bf16[1536,256]{1,0:T(8,128)(2,1)} %copy-done.13) | copy-start | bytes 2359300
  497.6 159.5 %copy-start.16 = (bf16[3,512,256]{2,1,0:T(8,128)(2,1)S(1)}, bf16[3,512,256]{2,1,0:T(8,128)(2,1)}, u32[]{:S(2)}) copy-start(bf16[3,512,256]{2,1,0:T(8,128)(2,1)} %copy-done.15) | copy-start | bytes 2359300
  497.6 192.6 %all-gather.11.cloned.1.call-start = ((), (), s32[]{:S(2)}) async-start(), calls=%async_computation.4 | async-start | bytes 1474560 | tf_op jit(solution)/shard_map/all_gather | solution.py:361
  562.0 143.6 %all-gather.13.cloned.1.call-start = ((), (), s32[]{:S(2)}) async-start(), calls=%async_computation.5 | async-start | bytes 2785280 | tf_op jit(solution)/shard_map/all_gather | solution.py:321
  659.4 2.4 collective-permute-start.25
  660.3 4.6 collective-permute-start.24
  662.6 26.0 %copy-start.12 = (f32[384,1024]{1,0:T(8,128)S(1)}, f32[384,1024]{1,0:T(8,128)}, u32[]{:S(2)}) copy-start(f32[384,1024]{1,0:T(8,128)} %get-tuple-element.397) | copy-start | bytes 4718596
  662.6 26.0 %collective-permute-start.26 = (bf16[384,1024]{1,0:T(8,128)(2,1)S(1)}, bf16[384,1024]{1,0:T(8,128)(2,1)S(1)}, u32[]{:S(2)}, u32[]{:S(2)}) collective-permute-start(bf16[384,1024]{1,0:T(8,128)(2,1)S(1)} %add_convert_fusion), channel_id=1, source_target_pairs={{0,2},{1,3},{2,0},{3,1},{4,6},{5,7},{6,4},{7,5},{8,10},{9,11},{10,... | collective-permute-start | bytes 2359304 | tf_op jit(solution)/shard_map/ppermute | solution.py:16
  (69 other events, 413.0 us)
Sparse Core Ops, SparseCore 0:
  10.8 49.1 all-gather.6
  62.7 97.3 all-gather.8
  491.0 69.0 reduce-scatter.6
  563.6 91.3 reduce-scatter.8
  657.0 23.6 all-gather.10
  682.0 23.5 all-gather.12
